TPU v7x, 256 devices: a whole 4x4x8 slice. The times are simulated.
256 devices in a mesh: dp: 8 (over z), seq: 32 (over x, y, core).
Axes of the slice: x: 4, y: 4, z: 8, core: 2. Of those that a mesh axis runs over, the one named last changes fastest.
Arguments:
- tokens: bfloat16 [8, 12288, 4096], P('dp', 'seq'), may hold values from -16 to 16
- qkv_weight: bfloat16 [4096, 3072], P(('dp', 'seq')), may hold values from -1 to 1
- segments: int32 [8, 12288], P('dp', 'seq'), may hold values from 0 to 12287, as said below
- destination: int32 [8, 12288], P('dp', 'seq'), may hold values from 0 to 12287, as said below
- doc_prefix: int32 [8, 32], P('dp', 'seq'), may hold values from 0 to 768, as said below
Outputs:
- attended: bfloat16 [8, 12288, 2048], P('dp', 'seq')
Inputs may be any that keep to these rules, and one draw needn't show every extreme that they name: `segments`: A token's id is the position in its sequence of its document's first token, so ids never fall and start at 0; the last token of every sequence is a document of its own. doc_prefix[b, d] is the number of tokens before row d * 384 of sequence b with that row's segment id; the most is reached in every draw. `destination`: each row is a permutation; the tokens of one device go to exactly 16 devices of the sequence, exactly 24 to each, and every device receives tokens from exactly 16 devices.
All inputs are finite; a program needn't handle non-finite values.
Results may differ from a plain program's by a relative error of at most 0.012.
The roundings to bfloat16 on the way count: a program that leaves them out, or rounds other values in their place, can miss the bound.
Values may be sent and summed in bfloat16 or wider, within the bound.
No kernel may reach another device: no remote copies, remote signals or barrier semaphores. Data moves between devices by JAX's collectives and lax.ppermute only.
A program may use at most 128 MiB of HBM per device.

v0:
```python
import jax
import jax.numpy as jnp
from jax import lax
from jax.experimental import pallas as pl
from jax.experimental.pallas import tpu as pltpu
from jax.sharding import Mesh, PartitionSpec as P


HEADS = 16
KV_HEADS = 4
HEAD_DIM = 128
REACH = 2
ROPE_BASE = 500000.0
MASKED = -1e30
LOG2E = 1.4426950408889634

NZ, NX, NY, NC = 8, 4, 4, 2
NCHIP = NX * NY
TOK = 384
CAP = 24
D = 4096
DEV = NCHIP * NC
PART = 512


bf16 = jnp.bfloat16
f32 = jnp.float32


def shift(x, axis, n, d):
    return lax.ppermute(x, axis, [(i, (i + d) % n) for i in range(n)])


OFFSETS_Z = (0, 1, 7, 3, 4, 2, 5, 6)
OFFSETS_C = (0, 1, 7, 2, 6, 3, 5, 4)


def each(pair, axis, n):
    return [shift(pair[0], axis, n, 1), shift(pair[1], axis, n, -1)]


def positions(segment_ids, prefix_len):
    index_list = jnp.arange(segment_ids.shape[0], dtype=jnp.int32)
    fresh_doc = jnp.concatenate([jnp.ones((1,), jnp.bool_), segment_ids[1:] != segment_ids[:-1]])
    first_row = lax.cummax(jnp.where(fresh_doc, index_list, 0), axis=0)
    leading = segment_ids == segment_ids[0]
    return index_list - first_row + jnp.where(leading, prefix_len, 0)


def assemble_kernel(zs_ref, one_ref, up_ref, down_ref, up3_ref, down3_ref, out_ref):
    pieces = [one_ref[...], up_ref[...], down_ref[...]]
    pieces += [up3_ref[k] for k in range(3)] + [down3_ref[k] for k in range(2)]
    for k, x in enumerate(pieces):
        out_ref[zs_ref[k]] = x


def assemble(zs, *pieces):
    vm = pl.BlockSpec(memory_space=pltpu.VMEM)
    return pl.pallas_call(
        assemble_kernel,
        out_shape=jax.ShapeDtypeStruct((NZ, 32, 2 * PART), bf16),
        in_specs=[pl.BlockSpec(memory_space=pltpu.SMEM)] + [vm] * len(pieces),
        out_specs=vm,
        cost_estimate=SMALL,
        name="assemble",
    )(zs, *pieces)


SMALL = pl.CostEstimate(flops=1 << 20, bytes_accessed=1 << 20, transcendentals=0)
HALF = PART // 2


def finish(acc, rotary, cos_ref, sin_ref, out_ref, b):
    for h in range(HALF // HEAD_DIM):
        x = acc[:, h * HEAD_DIM : (h + 1) * HEAD_DIM]
        if h < rotary:
            x = x * cos_ref[b] + pltpu.roll(x, HEAD_DIM // 2, 1) * sin_ref[b]
        out_ref[b, :, h * HEAD_DIM : (h + 1) * HEAD_DIM] = x.astype(bf16)


def project_kv_kernel(lane_ref, own_ref, other_ref, *refs):
    *w_refs, cos_ref, sin_ref, first_ref, second_ref = refs
    depth = D // NZ
    for n in range(2):
        cols = slice(n * HALF, (n + 1) * HALF)
        for b, ref in enumerate((own_ref, other_ref)):
            acc = None
            for k in range(NZ):
                w = w_refs[k][:, cols] if k < NZ - 1 else w_refs[NZ - 1 + n][...]
                tok = ref[:, pl.ds(pl.multiple_of(lane_ref[k], depth), depth)]
                term = jnp.dot(tok, w, preferred_element_type=f32)
                acc = term if acc is None else acc + term
            finish(acc, 1, cos_ref, sin_ref, (first_ref, second_ref)[n], b)


def project_kv(lanes, *arrays):
    vm = pl.BlockSpec(memory_space=pltpu.VMEM)
    return pl.pallas_call(
        project_kv_kernel,
        out_shape=[jax.ShapeDtypeStruct((2, TOK, HALF), bf16)] * 2,
        in_specs=[pl.BlockSpec(memory_space=pltpu.SMEM)] + [vm] * len(arrays),
        out_specs=[vm, vm],
        cost_estimate=SMALL,
        name="project_kv",
    )(lanes, *arrays)


def project_q_kernel(own_ref, other_ref, w_ref, cos_ref, sin_ref, out_ref):
    depth = D // NZ
    for b, ref in enumerate((own_ref, other_ref)):
        acc = None
        for z in range(NZ):
            w = w_ref[:, z].reshape(depth, HALF)
            term = jnp.dot(ref[:, z * depth : (z + 1) * depth], w, preferred_element_type=f32)
            acc = term if acc is None else acc + term
        finish(acc, 2, cos_ref, sin_ref, out_ref, b)


def project_q(head, own, other, w, cosine, sine):
    tok = pl.BlockSpec((TOK, D), lambda n: (0, 0))
    ang = pl.BlockSpec((2, TOK, HEAD_DIM), lambda n: (0, 0, 0))
    return pl.pallas_call(
        project_q_kernel,
        out_shape=jax.ShapeDtypeStruct((2, TOK, PART), bf16),
        grid=(2,),
        in_specs=[
            tok, tok, pl.BlockSpec((NCHIP, NZ, 32, HALF), lambda n: (0, 0, 0, 2 * head + n)), ang, ang
        ],
        out_specs=pl.BlockSpec((2, TOK, HALF), lambda n: (0, 0, n)),
        cost_estimate=SMALL,
        name="project_q",
    )(own, other, w, cosine, sine)


GROUP = HEADS // KV_HEADS
TILE = 128


def attend_kernel(
    info_ref, q_ref, cur_ref, prev_ref, segc_ref, segr_ref, slot_ref, out_ref, kv_ref, bias_ref, rows_ref
):
    b = pl.program_id(0)
    core = info_ref[0]
    i = jnp.bitwise_xor(core, b)
    span = REACH * TOK

    @pl.when(b == 0)
    def _():
        for n in range(2):
            k = jnp.bitwise_xor(core, n)
            for m, ref in ((n, prev_ref), (2 + n, cur_ref)):
                kv_ref[m, :, : 2 * HEAD_DIM] = ref[k]
                kv_ref[m, :, 2 * HEAD_DIM :] = jnp.ones((TOK, HEAD_DIM), bf16)

    prefix = info_ref[1 + i]
    segc = segc_ref[i]
    segr = segr_ref[i]
    leading = segc == segr[:, :1]
    row = lax.broadcasted_iota(jnp.int32, (TOK, TOK), 0)
    col = lax.broadcasted_iota(jnp.int32, (TOK, TOK), 1)
    bias_ref[:, span:] = jnp.where((col <= row) & (segc == segr), 0.0, MASKED)
    rcol = lax.broadcasted_iota(jnp.int32, (TOK, span), 1) - span
    bias_ref[:, :span] = jnp.where((rcol >= -prefix) & leading, 0.0, MASKED)

    keys = kv_ref[pl.ds(b, 3), :, :HEAD_DIM].reshape(3 * TOK, HEAD_DIM)
    vals = kv_ref[pl.ds(b, 3), :, HEAD_DIM:].reshape(3 * TOK, 2 * HEAD_DIM)
    for r in range(TOK // TILE):
        rows = slice(r * TILE, (r + 1) * TILE)
        n = span + (r + 1) * TILE
        for g in range(GROUP):
            cols = slice(g * HEAD_DIM, (g + 1) * HEAD_DIM)
            s = lax.dot_general(
                q_ref[i, rows, cols], keys[:n], (((1,), (1,)), ((), ())), preferred_element_type=f32
            )
            s = s * (HEAD_DIM**-0.5 * LOG2E) + bias_ref[rows, :n]
            e = jnp.exp2(s - jnp.max(s, axis=1, keepdims=True)).astype(bf16)
            o = jnp.dot(e, vals[:n], preferred_element_type=f32)
            rows_ref[rows, cols] = (o[:, :HEAD_DIM] / o[:, HEAD_DIM:]).astype(bf16)

    slots = lax.broadcasted_iota(jnp.int32, (DEV * CAP, TOK), 0)
    pick = jnp.where(slots == slot_ref[i], 1.0, 0.0).astype(bf16)
    packed = jnp.dot(pick, rows_ref[...], preferred_element_type=f32)
    out_ref[:, 0] = packed.reshape(DEV, CAP, GROUP * HEAD_DIM).astype(bf16)


def attend(q, cur, prev, info, segc, segr, slot):
    width = GROUP * HEAD_DIM

    def whole(x):
        return pl.BlockSpec(x.shape, lambda b, info: (0,) * x.ndim)

    return pl.pallas_call(
        attend_kernel,
        out_shape=jax.ShapeDtypeStruct((DEV, 2, CAP, width), bf16),
        grid_spec=pltpu.PrefetchScalarGridSpec(
            num_scalar_prefetch=1,
            grid=(2,),
            in_specs=[
                whole(q), whole(cur), whole(prev), whole(segc), whole(segr), whole(slot),
            ],
            out_specs=pl.BlockSpec((DEV, 1, CAP, width), lambda b, info: (0, b, 0, 0)),
            scratch_shapes=[
                pltpu.VMEM((4, TOK, 3 * HEAD_DIM), bf16),
                pltpu.VMEM((TOK, 3 * TOK), f32),
                pltpu.VMEM((TOK, width), bf16),
            ],
        ),
        cost_estimate=SMALL,
        name="attend",
    )(info, q, cur, prev, segc, segr, slot)


def place_kernel(places_ref, first_ref, second_ref, out_ref, pick_ref):
    step = pl.program_id(0)

    @pl.when(step == 0)
    def _():
        rows = lax.broadcasted_iota(jnp.int32, (TOK, DEV * CAP), 0)
        pick_ref[...] = jnp.where(rows == places_ref[...], 1.0, 0.0).astype(bf16)

    for j, ref in enumerate((first_ref, second_ref)):
        got = ref[...].reshape(DEV * CAP, PART)
        out_ref[:, j * PART : (j + 1) * PART] = jnp.dot(
            pick_ref[...], got, preferred_element_type=f32
        ).astype(bf16)


def place(places, first, second):
    spec = pl.BlockSpec((NCHIP, 1, NC * CAP, PART), lambda c: (0, c, 0, 0))
    return pl.pallas_call(
        place_kernel,
        out_shape=jax.ShapeDtypeStruct((TOK, HEADS * HEAD_DIM), bf16),
        grid=(NC,),
        in_specs=[pl.BlockSpec((1, DEV * CAP), lambda c: (0, 0)), spec, spec],
        out_specs=pl.BlockSpec((TOK, 2 * PART), lambda c: (0, c)),
        scratch_shapes=[pltpu.VMEM((TOK, DEV * CAP), bf16)],
        cost_estimate=SMALL,
        name="place",
    )(places, first, second)


def on_device(tokens, qkv_weight, segments, destination, doc_prefix):
    own = tokens[0]
    core = lax.axis_index("core")
    plane = ("x", "y", "core")
    chips = ("x", "y")

    qw, kw = HEADS * HEAD_DIM // NC, KV_HEADS * HEAD_DIM // NC

    def kv_half(c):
        first = [NC * qw + c * kw + h * HEAD_DIM + v * NC * kw for h in range(2) for v in range(2)]
        return jnp.concatenate(
            [lax.dynamic_slice_in_dim(qkv_weight, f, HEAD_DIM, 1) for f in first], axis=1
        )

    def q_half(c):
        return lax.dynamic_slice_in_dim(qkv_weight, c * qw, qw, 1)

    def by_core(x, y):
        return jnp.where(core == 0, jnp.concatenate([x, y]), jnp.concatenate([y, x]))

    def swapped(half):
        return by_core(half(core), shift(half(1 - core), "core", NC, 1))

    w = swapped(lambda c: jnp.concatenate([kv_half(c), q_half(c)], axis=1))
    wc, wab = w[:, :PART], w[:, PART:]
    other = shift(own, "core", NC, 1)

    seg = segments[0]
    prefix = doc_prefix[0, 0]
    target = destination[0]
    owner = target // TOK
    one_hot = (owner[:, None] == jnp.arange(DEV, dtype=jnp.int32)[None, :]).astype(jnp.int32)
    rank = jnp.sum(jnp.cumsum(one_hot, axis=0) * one_hot, axis=1) - 1
    slot = owner * CAP + rank
    table = jnp.stack(
        [positions(seg, prefix), seg, slot, target % TOK, jnp.broadcast_to(prefix, seg.shape)]
    )
    tables = jnp.stack([table, shift(table, "core", NC, 1)])
    pos, segs, slots, rows, prefixes = (tables[:, k] for k in range(5))
    hit = slots[:, None, :] == jnp.arange(DEV * CAP, dtype=jnp.int32)[None, :, None]
    send = jnp.sum(jnp.where(hit, rows[:, None, :], 0), axis=2).reshape(2, NCHIP, NC, CAP)
    send = lax.dynamic_index_in_dim(send, core, 2, keepdims=False)
    send = jnp.where(core == 0, send, send[::-1]).transpose(1, 0, 2).reshape(NCHIP, NC * CAP)
    send = jnp.concatenate([send // 16, send % 16], axis=1).astype(bf16)
    send = jnp.pad(send[:, None, :], ((0, 0), (0, 15), (0, PART - 2 * NC * CAP)))
    frequency = ROPE_BASE ** (
        -2.0 * jnp.arange(HEAD_DIM // 2, dtype=f32) / HEAD_DIM
    )
    angles = pos.astype(f32)[:, :, None] * frequency[None, None, :]
    cosine, sine = jnp.cos(angles), jnp.sin(angles)
    cosine = jnp.concatenate([cosine, cosine], axis=2)
    sine = jnp.concatenate([-sine, sine], axis=2)
    info = jnp.concatenate([core.reshape(1).astype(jnp.int32), prefixes[:, 0]])
    segc, segr, slots = segs[:, :, None], segs[:, None, :], slots[:, None, :]

    zi = lax.axis_index("dp").astype(jnp.int32)
    z_ab = (zi - jnp.array(OFFSETS_Z, jnp.int32)) % NZ
    lanes = (zi - jnp.array(OFFSETS_C, jnp.int32)) % NZ * (D // NZ)

    tie = lax.optimization_barrier
    up, down = shift(wab, "dp", NZ, 1), shift(wab, "dp", NZ, -1)
    up, down, wc = tie((up, down, wc))
    up3 = shift(jnp.stack([wab, up, down]), "dp", NZ, 3)
    down3 = shift(jnp.stack([wab, up]), "dp", NZ, -3)
    wz = assemble(z_ab, wab, up, down, up3, down3)
    wq = lax.all_gather(wz.reshape(NZ * 32, 2 * PART), chips, axis=0, tiled=True)

    first = jnp.concatenate([jnp.broadcast_to(wc[None], (NCHIP, *wc.shape)), send], axis=1)
    first = lax.all_to_all(first, chips, split_axis=0, concat_axis=0, tiled=True)
    c0 = first[:, :32].reshape(D // NZ, PART)
    places = first[:, 32, : 2 * NC * CAP].astype(jnp.int32)
    places = (places[:, : NC * CAP] * 16 + places[:, NC * CAP :]).reshape(1, DEV * CAP)
    c1 = each([c0, c0], "dp", NZ)
    c2 = each(c1, "dp", NZ)
    c3 = each(c2, "dp", NZ)
    c4 = each([c3[0][:, :HALF], c3[1][:, HALF:]], "dp", NZ)
    cur = project_kv(lanes, own, other, c0, *c1, *c2, *c3, *c4, cosine, sine)
    onward = [(i, i + 1) for i in range(NCHIP - 1)]
    prev = []
    for h in range(2):
        prev.append(lax.ppermute(cur[h], chips, onward))
    wq = wq.reshape(NCHIP, NZ, 32, 2 * PART)

    got = []
    for head in range(2):
        q = project_q(head, own, other, wq, cosine, sine)
        packed = attend(q, cur[head], prev[head], info, segc, segr, slots)
        got.append(
            lax.all_to_all(
                packed.reshape(DEV, NC * CAP, PART), plane, split_axis=0, concat_axis=0, tiled=True
            ).reshape(NCHIP, NC, NC * CAP, PART)
        )
    return place(places, got[0], got[1])[None]


def solution(mesh):
    grid = Mesh(mesh.devices.reshape(NZ, NX, NY, NC), ("dp", "x", "y", "core"))
    seq = ("x", "y", "core")
    placed = (P("dp", seq, None), P(("dp", *seq), None), P("dp", seq), P("dp", seq), P("dp", seq))

    return jax.shard_map(
        on_device, mesh=grid, in_specs=placed, out_specs=P("dp", seq, None), check_vma=False
    )
```

profile of v0, /device:TPU:1, one launch (start us, length us, event | category | flops | bytes accessed | tf_op | source)
XLA Modules:
  0.0 243.2 jit_solution(15139668325667550169)
XLA Ops:
  11.0 3.2 %collective-permute-start = (bf16[16,1536]{1,0:T(8,128)(2,1)S(1)}, bf16[16,1536]{1,0:T(8,128)(2,1)S(1)}, u32[]{:S(2)}, u32[]{:S(2)}) collective-permute-start(bf16[16,1536]{1,0:T(8,128)(2,1)S(1)} %get-tuple-element.20), channel_id=1, source_target_pairs={{0,1},{1,0},{2,3},{3,2},{4,5},{5,4},{6,7},{7,6},{8,9},{9,8},{10,11... | collective-permute-start | bytes 147464 | tf_op jit(solution)/shard_map/ppermute | solution.py:31
  15.2 3.9 %collective-permute-start.2 = (bf16[32,1024]{1,0:T(8,128)(2,1)S(1)}, bf16[32,1024]{1,0:T(8,128)(2,1)S(1)}, u32[]{:S(2)}, u32[]{:S(2)}) collective-permute-start(bf16[32,1024]{1,0:T(8,128)(2,1)S(1)} %get-tuple-element.18.one_ref), channel_id=1, source_target_pairs={{0,224},{32,0},{64,32},{96,64},{128,96},{160,128},{192,160},{224,1... | collective-permute-start | bytes 196616 | tf_op jit(solution)/shard_map/ppermute | solution.py:31
  20.4 3.0 %collective-permute-done.1.up_ref = bf16[32,1024]{1,0:T(8,128)(2,1)S(1)} collective-permute-done((bf16[32,1024]{1,0:T(8,128)(2,1)S(1)}, bf16[32,1024]{1,0:T(8,128)(2,1)S(1)}, u32[]{:S(2)}, u32[]{:S(2)}) %collective-permute-start.1) | collective-permute-done | bytes 65568 | tf_op jit(solution)/shard_map/ppermute | solution.py:31
  24.3 2.6 %collective-permute-start.5 = (bf16[3,32,1024]{2,1,0:T(8,128)(2,1)S(1)}, bf16[3,32,1024]{2,1,0:T(8,128)(2,1)}, u32[]{:S(2)}, u32[]{:S(2)}) collective-permute-start(bf16[3,32,1024]{2,1,0:T(8,128)(2,1)S(1)} %pad_maximum_fusion.2), channel_id=1, source_target_pairs={{0,96},{32,128},{64,160},{96,192},{128,224},{160,0},{192,32},{224,... | collective-permute-start | bytes 589832 | tf_op jit(solution)/shard_map/ppermute | solution.py:31
  28.0 4.4 %collective-permute-done.6.down3_ref = bf16[2,32,1024]{2,1,0:T(8,128)(2,1)S(1)} collective-permute-done((bf16[2,32,1024]{2,1,0:T(8,128)(2,1)S(1)}, bf16[2,32,1024]{2,1,0:T(8,128)(2,1)S(1)}, u32[]{:S(2)}, u32[]{:S(2)}) %collective-permute-start.6) | collective-permute-done | bytes 131104 | tf_op jit(solution)/shard_map/ppermute | solution.py:31
  33.1 1.9 assemble.1
  39.0 6.5 %collective-permute-start.3 = (s32[5,384]{1,0:T(8,128)S(1)}, s32[5,384]{1,0:T(8,128)S(1)}, u32[]{:S(2)}, u32[]{:S(2)}) collective-permute-start(s32[5,384]{1,0:T(8,128)S(1)} %stack.32), channel_id=1, source_target_pairs={{0,1},{1,0},{2,3},{3,2},{4,5},{5,4},{6,7},{7,6},{8,9},{9,8},{10,11... | collective-permute-start | bytes 23048 | tf_op jit(solution)/shard_map/ppermute | solution.py:31
  47.2 24.8 %all_to_all.15 = bf16[16,48,512]{2,1,0:T(8,128)(2,1)S(1)} all-to-all(bf16[16,48,512]{2,1,0:T(8,128)(2,1)S(1)} %fusion.1), channel_id=1, replica_groups=mesh['dp'=8,'x'=4,'y'=4,'core'=2] {'x','y'}, dimensions={0} | all-to-all | bytes 1572864 | tf_op jit(solution)/shard_map/all_to_all | solution.py:310
  72.1 4.5 %collective-permute-start.8 = (bf16[512,512]{1,0:T(8,128)(2,1)S(1)}, bf16[512,512]{1,0:T(8,128)(2,1)S(1)}, u32[]{:S(2)}, u32[]{:S(2)}) collective-permute-start(bf16[512,512]{1,0:T(8,128)(2,1)S(1)} %bitcast.86), channel_id=1, source_target_pairs={{0,224},{32,0},{64,32},{96,64},{128,96},{160,128},{192,160},{224,1... | collective-permute-start | bytes 1572872 | tf_op jit(solution)/shard_map/ppermute | solution.py:31
  77.3 10.2 %collective-permute-done.8.refs_2_ = bf16[512,512]{1,0:T(8,128)(2,1)S(1)} collective-permute-done((bf16[512,512]{1,0:T(8,128)(2,1)S(1)}, bf16[512,512]{1,0:T(8,128)(2,1)S(1)}, u32[]{:S(2)}, u32[]{:S(2)}) %collective-permute-start.8) | collective-permute-done | bytes 524320 | tf_op jit(solution)/shard_map/ppermute | solution.py:31
  90.1 10.1 %collective-permute-done.10.refs_4_ = bf16[512,512]{1,0:T(8,128)(2,1)S(1)} collective-permute-done((bf16[512,512]{1,0:T(8,128)(2,1)S(1)}, bf16[512,512]{1,0:T(8,128)(2,1)S(1)}, u32[]{:S(2)}, u32[]{:S(2)}) %collective-permute-start.10) | collective-permute-done | bytes 524320 | tf_op jit(solution)/shard_map/ppermute | solution.py:31
  102.3 8.7 %collective-permute-done.12.refs_6_ = bf16[512,512]{1,0:T(8,128)(2,1)S(1)} collective-permute-done((bf16[512,512]{1,0:T(8,128)(2,1)S(1)}, bf16[512,512]{1,0:T(8,128)(2,1)S(1)}, u32[]{:S(2)}, u32[]{:S(2)}) %collective-permute-start.12) | collective-permute-done | bytes 524320 | tf_op jit(solution)/shard_map/ppermute | solution.py:31
  118.3 8.5 %project_kv.1 = (bf16[2,384,256]{2,1,0:T(8,128)(2,1)}, bf16[2,384,256]{2,1,0:T(8,128)(2,1)}) custom-call(s32[8]{0:T(128)} %fusion.19.lane_ref, bf16[384,4096]{1,0:T(8,128)(2,1)} %bitcast.78, bf16[384,4096]{1,0:T(8,128)(2,1)} %collective-permute-done.4.other_ref, bf16[512,512]{1,0:T(8,128)(2,1)} %bitcast.88, bf16[512,512]{1,0:T(8,128)(2,1)} %copy-done.9, ...), custom_call_target="tpu_custom_call" | custom-call | flops 1048576 | bytes 1048576 | tf_op jit(solution)/shard_map/project_kv/pallas_call | solution.py:98
  126.8 3.8 %collective-permute-start.15 = (bf16[2,384,256]{2,1,0:T(8,128)(2,1)}, bf16[2,384,256]{2,1,0:T(8,128)(2,1)S(1)}, u32[]{:S(2)}, u32[]{:S(2)}) collective-permute-start(bf16[2,384,256]{2,1,0:T(8,128)(2,1)} %get-tuple-element.13.cur_ref), channel_id=1, source_target_pairs={{0,2},{2,4},{4,6},{6,8},{8,10},{10,12},{12,14},{14,16},{16,18},{18... | collective-permute-start | bytes 1179656 | tf_op jit(solution)/shard_map/ppermute | solution.py:322
  132.3 8.4 %project_q.2.q_ref = bf16[2,384,512]{2,1,0:T(8,128)(2,1)} custom-call(bf16[384,4096]{1,0:T(8,128)(2,1)} %bitcast.79, bf16[384,4096]{1,0:T(8,128)(2,1)} %collective-permute-done.4.other_ref, bf16[16,8,32,1024]{3,2,1,0:T(8,128)(2,1)} %bitcast.76, f32[2,384,128]{2,1,0:T(8,128)} %pad_maximum_fusion.cos_ref.refs_9_, f32[2,384,128]{2,1,0:T(8,128)} %pad_maximum_fusion.1.sin_ref.refs_10_), custom_call_target="tpu_custom_call" | custom-call | flops 1048576 | bytes 1048576 | tf_op jit(solution)/shard_map/project_q/pallas_call | solution.py:122
  141.5 9.7 %attend.2 = bf16[32,2,24,512]{3,2,1,0:T(8,128)(2,1)} custom-call(s32[3]{0:T(128)} %pad_add_fusion.4.info_ref, bf16[2,384,512]{2,1,0:T(8,128)(2,1)} %project_q.2.q_ref, bf16[2,384,256]{2,1,0:T(8,128)(2,1)} %get-tuple-element.13.cur_ref, bf16[2,384,256]{2,1,0:T(8,128)(2,1)} %copy-done.13, s32[2,384,1]{2,1,0:T(8,128)} %copy.34.segc_ref, ...), custom_call_target="tpu_custom_call" | custom-call | flops 1048576 | bytes 1048576 | tf_op jit(solution)/shard_map/attend/pallas_call | solution.py:192
  151.1 11.5 %all-to-all-start.1 = ((bf16[32,48,512]{2,1,0:T(8,128)(2,1)}), bf16[32,48,512]{2,1,0:T(8,128)(2,1)S(1)}, u32[]{:S(2)}, u32[]{:S(2)}) async-start(bf16[32,48,512]{2,1,0:T(8,128)(2,1)} %bitcast.83), calls=%async_computation.1 | async-start | bytes 3145728 | tf_op jit(solution)/shard_map/all_to_all | solution.py:330
  162.6 3.5 %collective-permute-start.16 = (bf16[2,384,256]{2,1,0:T(8,128)(2,1)S(1)}, bf16[2,384,256]{2,1,0:T(8,128)(2,1)S(1)}, u32[]{:S(2)}, u32[]{:S(2)}) collective-permute-start(bf16[2,384,256]{2,1,0:T(8,128)(2,1)S(1)} %copy-done.12), channel_id=1, source_target_pairs={{0,2},{2,4},{4,6},{6,8},{8,10},{10,12},{12,14},{14,16},{16,18},{18... | collective-permute-start | bytes 1179656 | tf_op jit(solution)/shard_map/ppermute | solution.py:322
  166.1 8.4 %project_q.3.q_ref = bf16[2,384,512]{2,1,0:T(8,128)(2,1)} custom-call(bf16[384,4096]{1,0:T(8,128)(2,1)} %bitcast.80, bf16[384,4096]{1,0:T(8,128)(2,1)} %collective-permute-done.4.other_ref, bf16[16,8,32,1024]{3,2,1,0:T(8,128)(2,1)} %bitcast.77, f32[2,384,128]{2,1,0:T(8,128)} %pad_maximum_fusion.cos_ref.refs_9_, f32[2,384,128]{2,1,0:T(8,128)} %pad_maximum_fusion.1.sin_ref.refs_10_), custom_call_target="tpu_custom_call" | custom-call | flops 1048576 | bytes 1048576 | tf_op jit(solution)/shard_map/project_q/pallas_call | solution.py:122
  174.6 13.6 %collective-permute-done.16.prev_ref = bf16[2,384,256]{2,1,0:T(8,128)(2,1)S(1)} collective-permute-done((bf16[2,384,256]{2,1,0:T(8,128)(2,1)S(1)}, bf16[2,384,256]{2,1,0:T(8,128)(2,1)S(1)}, u32[]{:S(2)}, u32[]{:S(2)}) %collective-permute-start.16) | collective-permute-done | bytes 393248 | tf_op jit(solution)/shard_map/ppermute | solution.py:322
  188.9 9.7 %attend.3 = bf16[32,2,24,512]{3,2,1,0:T(8,128)(2,1)} custom-call(s32[3]{0:T(128)} %pad_add_fusion.4.info_ref, bf16[2,384,512]{2,1,0:T(8,128)(2,1)} %project_q.3.q_ref, bf16[2,384,256]{2,1,0:T(8,128)(2,1)} %get-tuple-element.14.cur_ref, bf16[2,384,256]{2,1,0:T(8,128)(2,1)} %copy-done.14, s32[2,384,1]{2,1,0:T(8,128)} %copy.34.segc_ref, ...), custom_call_target="tpu_custom_call" | custom-call | flops 1048576 | bytes 1048576 | tf_op jit(solution)/shard_map/attend/pallas_call | solution.py:192
  199.8 8.8 %all-to-all-start.2 = ((bf16[32,48,512]{2,1,0:T(8,128)(2,1)}), bf16[32,48,512]{2,1,0:T(8,128)(2,1)S(1)}, u32[]{:S(2)}, u32[]{:S(2)}) async-start(bf16[32,48,512]{2,1,0:T(8,128)(2,1)} %bitcast.84), calls=%async_computation.2 | async-start | bytes 3145728 | tf_op jit(solution)/shard_map/all_to_all | solution.py:330
  210.1 21.1 %all-to-all-done.2 = bf16[32,48,512]{2,1,0:T(8,128)(2,1)S(1)} async-done(((bf16[32,48,512]{2,1,0:T(8,128)(2,1)}), bf16[32,48,512]{2,1,0:T(8,128)(2,1)S(1)}, u32[]{:S(2)}, u32[]{:S(2)}) %all-to-all-start.2) | async-done | bytes 1572896 | tf_op jit(solution)/shard_map/all_to_all | solution.py:330
  232.4 3.9 %place.1 = bf16[384,2048]{1,0:T(8,128)(2,1)} custom-call(s32[1,768]{1,0:T(1,128)} %reshape.192.places_ref, bf16[16,2,48,512]{3,2,1,0:T(8,128)(2,1)} %bitcast.82, bf16[16,2,48,512]{3,2,1,0:T(8,128)(2,1)} %bitcast.85), custom_call_target="tpu_custom_call" | custom-call | flops 1048576 | bytes 1048576 | tf_op jit(solution)/shard_map/place/pallas_call | solution.py:230
  (137 shorter events, 34.0 us)
Async XLA Ops:
  6.5 125.8 %all-gather.2.cloned.1.call-start = ((), (), s32[]{:S(2)}) async-start(), calls=%async_computation.3 | async-start | bytes 8912896 | tf_op jit(solution)/shard_map/all_gather | solution.py:307
  11.0 4.1 %collective-permute-start = (bf16[16,1536]{1,0:T(8,128)(2,1)S(1)}, bf16[16,1536]{1,0:T(8,128)(2,1)S(1)}, u32[]{:S(2)}, u32[]{:S(2)}) collective-permute-start(bf16[16,1536]{1,0:T(8,128)(2,1)S(1)} %get-tuple-element.20), channel_id=1, source_target_pairs={{0,1},{1,0},{2,3},{3,2},{4,5},{5,4},{6,7},{7,6},{8,9},{9,8},{10,11... | collective-permute-start | bytes 147464 | tf_op jit(solution)/shard_map/ppermute | solution.py:31
  15.2 5.3 %collective-permute-start.2 = (bf16[32,1024]{1,0:T(8,128)(2,1)S(1)}, bf16[32,1024]{1,0:T(8,128)(2,1)S(1)}, u32[]{:S(2)}, u32[]{:S(2)}) collective-permute-start(bf16[32,1024]{1,0:T(8,128)(2,1)S(1)} %get-tuple-element.18.one_ref), channel_id=1, source_target_pairs={{0,224},{32,0},{64,32},{96,64},{128,96},{160,128},{192,160},{224,1... | collective-permute-start | bytes 196616 | tf_op jit(solution)/shard_map/ppermute | solution.py:31
  19.1 4.3 %collective-permute-start.1 = (bf16[32,1024]{1,0:T(8,128)(2,1)S(1)}, bf16[32,1024]{1,0:T(8,128)(2,1)S(1)}, u32[]{:S(2)}, u32[]{:S(2)}) collective-permute-start(bf16[32,1024]{1,0:T(8,128)(2,1)S(1)} %get-tuple-element.18.one_ref), channel_id=1, source_target_pairs={{0,32},{32,64},{64,96},{96,128},{128,160},{160,192},{192,224},{224... | collective-permute-start | bytes 196616 | tf_op jit(solution)/shard_map/ppermute | solution.py:31
  23.5 8.9 %collective-permute-start.6 = (bf16[2,32,1024]{2,1,0:T(8,128)(2,1)S(1)}, bf16[2,32,1024]{2,1,0:T(8,128)(2,1)S(1)}, u32[]{:S(2)}, u32[]{:S(2)}) collective-permute-start(bf16[2,32,1024]{2,1,0:T(8,128)(2,1)S(1)} %pad_maximum_fusion.3), channel_id=1, source_target_pairs={{0,160},{32,192},{64,224},{96,0},{128,32},{160,64},{192,96},{224,1... | collective-permute-start | bytes 393224 | tf_op jit(solution)/shard_map/ppermute | solution.py:31
  24.3 8.8 %collective-permute-start.5 = (bf16[3,32,1024]{2,1,0:T(8,128)(2,1)S(1)}, bf16[3,32,1024]{2,1,0:T(8,128)(2,1)}, u32[]{:S(2)}, u32[]{:S(2)}) collective-permute-start(bf16[3,32,1024]{2,1,0:T(8,128)(2,1)S(1)} %pad_maximum_fusion.2), channel_id=1, source_target_pairs={{0,96},{32,128},{64,160},{96,192},{128,224},{160,0},{192,32},{224,... | collective-permute-start | bytes 589832 | tf_op jit(solution)/shard_map/ppermute | solution.py:31
  39.0 7.3 %collective-permute-start.3 = (s32[5,384]{1,0:T(8,128)S(1)}, s32[5,384]{1,0:T(8,128)S(1)}, u32[]{:S(2)}, u32[]{:S(2)}) collective-permute-start(s32[5,384]{1,0:T(8,128)S(1)} %stack.32), channel_id=1, source_target_pairs={{0,1},{1,0},{2,3},{3,2},{4,5},{5,4},{6,7},{7,6},{8,9},{9,8},{10,11... | collective-permute-start | bytes 23048 | tf_op jit(solution)/shard_map/ppermute | solution.py:31
  45.5 72.9 %collective-permute-start.4 = (bf16[384,4096]{1,0:T(8,128)(2,1)S(1)}, bf16[384,4096]{1,0:T(8,128)(2,1)}, u32[]{:S(2)}, u32[]{:S(2)}) collective-permute-start(bf16[384,4096]{1,0:T(8,128)(2,1)S(1)} %bitcast.81), channel_id=1, source_target_pairs={{0,1},{1,0},{2,3},{3,2},{4,5},{5,4},{6,7},{7,6},{8,9},{9,8},{10,11... | collective-permute-start | bytes 9437192 | tf_op jit(solution)/shard_map/ppermute | solution.py:31
  46.3 84.3 %copy-start.19 = (s32[2,1,384]{2,1,0:T(1,128)}, s32[2,1,384]{2,1,0:T(1,128)S(1)}, u32[]{:S(2)}) copy-start(s32[2,1,384]{2,1,0:T(1,128)S(1)} %get-tuple-element.27.segr_ref) | copy-start | bytes 9220
  47.2 54.5 %copy-start.23 = (s32[8]{0:T(128)S(1)}, s32[8]{0:T(128)}, u32[]{:S(2)}) copy-start(s32[8]{0:T(128)} %constant.155) | copy-start | bytes 100
  72.0 42.3 %copy-start.3 = (bf16[16,48,512]{2,1,0:T(8,128)(2,1)}, bf16[16,48,512]{2,1,0:T(8,128)(2,1)S(1)}, u32[]{:S(2)}) copy-start(bf16[16,48,512]{2,1,0:T(8,128)(2,1)S(1)} %all_to_all.15) | copy-start | bytes 2359300
  72.1 44.1 %copy-start.4 = (bf16[16,32,512]{2,1,0:T(8,128)(2,1)}, bf16[16,32,512]{2,1,0:T(8,128)(2,1)S(1)}, u32[]{:S(2)}) copy-start(bf16[16,32,512]{2,1,0:T(8,128)(2,1)S(1)} %slice.95) | copy-start | bytes 1572868
  72.1 15.4 %collective-permute-start.8 = (bf16[512,512]{1,0:T(8,128)(2,1)S(1)}, bf16[512,512]{1,0:T(8,128)(2,1)S(1)}, u32[]{:S(2)}, u32[]{:S(2)}) collective-permute-start(bf16[512,512]{1,0:T(8,128)(2,1)S(1)} %bitcast.86), channel_id=1, source_target_pairs={{0,224},{32,0},{64,32},{96,64},{128,96},{160,128},{192,160},{224,1... | collective-permute-start | bytes 1572872 | tf_op jit(solution)/shard_map/ppermute | solution.py:31
  76.6 12.0 %collective-permute-start.7 = (bf16[512,512]{1,0:T(8,128)(2,1)S(1)}, bf16[512,512]{1,0:T(8,128)(2,1)S(1)}, u32[]{:S(2)}, u32[]{:S(2)}) collective-permute-start(bf16[512,512]{1,0:T(8,128)(2,1)S(1)} %bitcast.87), channel_id=1, source_target_pairs={{0,32},{32,64},{64,96},{96,128},{128,160},{160,192},{192,224},{224... | collective-permute-start | bytes 1572872 | tf_op jit(solution)/shard_map/ppermute | solution.py:31
  87.5 12.6 %collective-permute-start.10 = (bf16[512,512]{1,0:T(8,128)(2,1)S(1)}, bf16[512,512]{1,0:T(8,128)(2,1)S(1)}, u32[]{:S(2)}, u32[]{:S(2)}) collective-permute-start(bf16[512,512]{1,0:T(8,128)(2,1)S(1)} %collective-permute-done.8.refs_2_), channel_id=1, source_target_pairs={{0,224},{32,0},{64,32},{96,64},{128,96},{160,128},{192,160},{224,1... | collective-permute-start | bytes 1572872 | tf_op jit(solution)/shard_map/ppermute | solution.py:31
  88.6 11.5 %collective-permute-start.9 = (bf16[512,512]{1,0:T(8,128)(2,1)S(1)}, bf16[512,512]{1,0:T(8,128)(2,1)S(1)}, u32[]{:S(2)}, u32[]{:S(2)}) collective-permute-start(bf16[512,512]{1,0:T(8,128)(2,1)S(1)} %collective-permute-done.7.refs_1_), channel_id=1, source_target_pairs={{0,32},{32,64},{64,96},{96,128},{128,160},{160,192},{192,224},{224... | collective-permute-start | bytes 1572872 | tf_op jit(solution)/shard_map/ppermute | solution.py:31
  100.1 10.9 %collective-permute-start.12 = (bf16[512,512]{1,0:T(8,128)(2,1)S(1)}, bf16[512,512]{1,0:T(8,128)(2,1)S(1)}, u32[]{:S(2)}, u32[]{:S(2)}) collective-permute-start(bf16[512,512]{1,0:T(8,128)(2,1)S(1)} %collective-permute-done.10.refs_4_), channel_id=1, source_target_pairs={{0,224},{32,0},{64,32},{96,64},{128,96},{160,128},{192,160},{224,1... | collective-permute-start | bytes 1572872 | tf_op jit(solution)/shard_map/ppermute | solution.py:31
  100.2 11.1 %collective-permute-start.11 = (bf16[512,512]{1,0:T(8,128)(2,1)S(1)}, bf16[512,512]{1,0:T(8,128)(2,1)S(1)}, u32[]{:S(2)}, u32[]{:S(2)}) collective-permute-start(bf16[512,512]{1,0:T(8,128)(2,1)S(1)} %collective-permute-done.9.refs_3_), channel_id=1, source_target_pairs={{0,32},{32,64},{64,96},{96,128},{128,160},{160,192},{192,224},{224... | collective-permute-start | bytes 1572872 | tf_op jit(solution)/shard_map/ppermute | solution.py:31
  111.1 6.0 %collective-permute-start.14 = (bf16[512,256]{1,0:T(8,128)(2,1)S(1)}, bf16[512,256]{1,0:T(8,128)(2,1)S(1)}, u32[]{:S(2)}, u32[]{:S(2)}) collective-permute-start(bf16[512,256]{1,0:T(8,128)(2,1)S(1)} %slice.97), channel_id=1, source_target_pairs={{0,224},{32,0},{64,32},{96,64},{128,96},{160,128},{192,160},{224,1... | collective-permute-start | bytes 786440 | tf_op jit(solution)/shard_map/ppermute | solution.py:31
  111.4 7.0 %collective-permute-start.13 = (bf16[512,256]{1,0:T(8,128)(2,1)S(1)}, bf16[512,256]{1,0:T(8,128)(2,1)}, u32[]{:S(2)}, u32[]{:S(2)}) collective-permute-start(bf16[512,256]{1,0:T(8,128)(2,1)S(1)} %slice.96), channel_id=1, source_target_pairs={{0,32},{32,64},{64,96},{96,128},{128,160},{160,192},{192,224},{224... | collective-permute-start | bytes 786440 | tf_op jit(solution)/shard_map/ppermute | solution.py:31
  126.8 13.9 %collective-permute-start.15 = (bf16[2,384,256]{2,1,0:T(8,128)(2,1)}, bf16[2,384,256]{2,1,0:T(8,128)(2,1)S(1)}, u32[]{:S(2)}, u32[]{:S(2)}) collective-permute-start(bf16[2,384,256]{2,1,0:T(8,128)(2,1)} %get-tuple-element.13.cur_ref), channel_id=1, source_target_pairs={{0,2},{2,4},{4,6},{6,8},{8,10},{10,12},{12,14},{14,16},{16,18},{18... | collective-permute-start | bytes 1179656 | tf_op jit(solution)/shard_map/ppermute | solution.py:322
  151.1 47.5 %all-to-all-start.1 = ((bf16[32,48,512]{2,1,0:T(8,128)(2,1)}), bf16[32,48,512]{2,1,0:T(8,128)(2,1)S(1)}, u32[]{:S(2)}, u32[]{:S(2)}) async-start(bf16[32,48,512]{2,1,0:T(8,128)(2,1)} %bitcast.83), calls=%async_computation.1 | async-start | bytes 3145728 | tf_op jit(solution)/shard_map/all_to_all | solution.py:330
  162.6 25.5 %collective-permute-start.16 = (bf16[2,384,256]{2,1,0:T(8,128)(2,1)S(1)}, bf16[2,384,256]{2,1,0:T(8,128)(2,1)S(1)}, u32[]{:S(2)}, u32[]{:S(2)}) collective-permute-start(bf16[2,384,256]{2,1,0:T(8,128)(2,1)S(1)} %copy-done.12), channel_id=1, source_target_pairs={{0,2},{2,4},{4,6},{6,8},{8,10},{10,12},{12,14},{14,16},{16,18},{18... | collective-permute-start | bytes 1179656 | tf_op jit(solution)/shard_map/ppermute | solution.py:322
  199.8 31.4 %all-to-all-start.2 = ((bf16[32,48,512]{2,1,0:T(8,128)(2,1)}), bf16[32,48,512]{2,1,0:T(8,128)(2,1)S(1)}, u32[]{:S(2)}, u32[]{:S(2)}) async-start(bf16[32,48,512]{2,1,0:T(8,128)(2,1)} %bitcast.84), calls=%async_computation.2 | async-start | bytes 3145728 | tf_op jit(solution)/shard_map/all_to_all | solution.py:330
  (20 other events, 232.5 us)
Sparse Core Ops, SparseCore 0:
  35.2 86.5 all-gather.1
where the time goes:
time: 244 us; the launch traced here: 243 us
  waiting for transfers between devices  76.1 us (31%)
  starting transfers between devices  55.7 us (23%)
  Pallas kernels  50.6 us (21%)
  blocking collectives  24.8 us (10%)
  between operations  14.4 us (6%)
  local copies, waits for them, and re-layouts  12.8 us (5%)
  other arithmetic  8.64 us (4%)
    ppermute x15, waiting for transfers between devices, shift(): return lax.ppermute(x, axis, [(i, (i + d) % n) for i in range(n)])  41.4 us
    ppermute x15, starting transfers between devices, shift(): return lax.ppermute(x, axis, [(i, (i + d) % n) for i in range(n)])  28.2 us
    all_to_all x1, blocking collectives, on_device(): lax.all_to_all(first, chips, split_axis=0, concat_axis=0, tiled=True)  24.8 us
    all_to_all x2, waiting for transfers between devices, on_device(): lax.all_to_all(packed.reshape(DEV, NC * CAP, PART), plane, split_axis=0,...  21.1 us
    all_to_all x2, starting transfers between devices, on_device(): lax.all_to_all(packed.reshape(DEV, NC * CAP, PART), plane, split_axis=0,...  20.2 us
    pallas_call x2, Pallas kernels, attend(): pl.pallas_call(attend_kernel, out_shape=jax.ShapeDtypeStruct((DEV, 2, CAP...  19.4 us
    pallas_call x2, Pallas kernels, project_q(): pl.pallas_call(project_q_kernel, out_shape=jax.ShapeDtypeStruct((2, TOK,...  16.8 us
    ppermute x2, waiting for transfers between devices, on_device(): prev.append(lax.ppermute(cur[h], chips, onward))  13.6 us
  transfers between devices with their start and end apart: 20, of which 12 were waited for; matrix products, arithmetic and copies ran while one was open for 5% of the time, Pallas kernels for 14%

commit v1 on v0

--- a/solution.py
+++ b/solution.py
@@ -31,7 +31,7 @@
     return lax.ppermute(x, axis, [(i, (i + d) % n) for i in range(n)])
 
 
-OFFSETS_Z = (0, 1, 7, 3, 4, 2, 5, 6)
+OFFSETS_Z = (0, 1, 7, 4, 2, 3, 6, 5)
 OFFSETS_C = (0, 1, 7, 2, 6, 3, 5, 4)
 
 
@@ -47,9 +47,50 @@
     return index_list - first_row + jnp.where(leading, prefix_len, 0)
 
 
-def assemble_kernel(zs_ref, one_ref, up_ref, down_ref, up3_ref, down3_ref, out_ref):
-    pieces = [one_ref[...], up_ref[...], down_ref[...]]
-    pieces += [up3_ref[k] for k in range(3)] + [down3_ref[k] for k in range(2)]
+def split_kernel(core_ref, w_ref, mine_ref, theirs_ref):
+    qw, kw = HEADS * HEAD_DIM // NC, KV_HEADS * HEAD_DIM // NC
+    for ref, c in ((mine_ref, core_ref[0]), (theirs_ref, 1 - core_ref[0])):
+        for h in range(2):
+            for v in range(2):
+                first = NC * qw + h * HEAD_DIM + v * NC * kw
+                at = (2 * h + v) * HEAD_DIM
+                ref[:, at : at + HEAD_DIM] = w_ref[
+                    :, pl.ds(pl.multiple_of(first + c * kw, HEAD_DIM), HEAD_DIM)
+                ]
+        ref[:, PART:] = w_ref[:, pl.ds(pl.multiple_of(c * qw, HEAD_DIM), qw)]
+
+
+def merge_kernel(core_ref, mine_ref, theirs_ref, c_ref, ab_ref):
+    rows = mine_ref.shape[0]
+    for ref, c in ((mine_ref, core_ref[0]), (theirs_ref, 1 - core_ref[0])):
+        at = pl.ds(pl.multiple_of(c * rows, rows), rows)
+        for p in range(NCHIP):
+            c_ref[p, at, :] = ref[:, :PART]
+        ab_ref[at, :] = ref[:, PART:]
+
+
+def small_call(kernel, shapes, scalars, *arrays):
+    vm = pl.BlockSpec(memory_space=pltpu.VMEM)
+    return pl.pallas_call(
+        kernel,
+        out_shape=[jax.ShapeDtypeStruct(x, bf16) for x in shapes],
+        in_specs=[pl.BlockSpec(memory_space=pltpu.SMEM)] + [vm] * len(arrays),
+        out_specs=[vm] * len(shapes),
+        cost_estimate=SMALL,
+    )(scalars, *arrays)
+
+
+def split(core_id, w):
+    return small_call(split_kernel, [(16, 3 * PART)] * 2, core_id, w)
+
+
+def merge(core_id, mine, theirs):
+    return small_call(merge_kernel, [(NCHIP, 32, PART), (32, 2 * PART)], core_id, mine, theirs)
+
+
+def assemble_kernel(zs_ref, one_ref, up_ref, down_ref, far_ref, up2_ref, down2_ref, out_ref):
+    pieces = [one_ref[...], up_ref[...], down_ref[...], far_ref[...]]
+    pieces += [r[k] for r in (up2_ref, down2_ref) for k in range(2)]
     for k, x in enumerate(pieces):
         out_ref[zs_ref[k]] = x
 
@@ -210,33 +251,35 @@
     )(info, q, cur, prev, segc, segr, slot)
 
 
-def place_kernel(places_ref, first_ref, second_ref, out_ref, pick_ref):
-    step = pl.program_id(0)
-
-    @pl.when(step == 0)
+def place_kernel(places_ref, got_ref, *refs):
+    out_ref, pick_ref = refs[-2:]
+
+    @pl.when(pl.program_id(0) == 0)
     def _():
         rows = lax.broadcasted_iota(jnp.int32, (TOK, DEV * CAP), 0)
         pick_ref[...] = jnp.where(rows == places_ref[...], 1.0, 0.0).astype(bf16)
 
-    for j, ref in enumerate((first_ref, second_ref)):
-        got = ref[...].reshape(DEV * CAP, PART)
-        out_ref[:, j * PART : (j + 1) * PART] = jnp.dot(
-            pick_ref[...], got, preferred_element_type=f32
-        ).astype(bf16)
-
-
-def place(places, first, second):
-    spec = pl.BlockSpec((NCHIP, 1, NC * CAP, PART), lambda c: (0, c, 0, 0))
+    out_ref[...] = jnp.dot(
+        pick_ref[...], got_ref[...].reshape(DEV * CAP, PART), preferred_element_type=f32
+    ).astype(bf16)
+
+
+def place(places, got, head, whole):
     return pl.pallas_call(
         place_kernel,
         out_shape=jax.ShapeDtypeStruct((TOK, HEADS * HEAD_DIM), bf16),
         grid=(NC,),
-        in_specs=[pl.BlockSpec((1, DEV * CAP), lambda c: (0, 0)), spec, spec],
-        out_specs=pl.BlockSpec((TOK, 2 * PART), lambda c: (0, c)),
+        in_specs=[
+            pl.BlockSpec((1, DEV * CAP), lambda c: (0, 0)),
+            pl.BlockSpec((NCHIP, 1, NC * CAP, PART), lambda c: (0, c, 0, 0)),
+        ]
+        + [pl.BlockSpec(memory_space=pl.ANY)] * len(whole),
+        out_specs=pl.BlockSpec((TOK, PART), lambda c: (0, 2 * c + head)),
         scratch_shapes=[pltpu.VMEM((TOK, DEV * CAP), bf16)],
+        input_output_aliases={2: 0} if whole else {},
         cost_estimate=SMALL,
         name="place",
-    )(places, first, second)
+    )(places, got, *whole)
 
 
 def on_device(tokens, qkv_weight, segments, destination, doc_prefix):
@@ -245,25 +288,9 @@
     plane = ("x", "y", "core")
     chips = ("x", "y")
 
-    qw, kw = HEADS * HEAD_DIM // NC, KV_HEADS * HEAD_DIM // NC
-
-    def kv_half(c):
-        first = [NC * qw + c * kw + h * HEAD_DIM + v * NC * kw for h in range(2) for v in range(2)]
-        return jnp.concatenate(
-            [lax.dynamic_slice_in_dim(qkv_weight, f, HEAD_DIM, 1) for f in first], axis=1
-        )
-
-    def q_half(c):
-        return lax.dynamic_slice_in_dim(qkv_weight, c * qw, qw, 1)
-
-    def by_core(x, y):
-        return jnp.where(core == 0, jnp.concatenate([x, y]), jnp.concatenate([y, x]))
-
-    def swapped(half):
-        return by_core(half(core), shift(half(1 - core), "core", NC, 1))
-
-    w = swapped(lambda c: jnp.concatenate([kv_half(c), q_half(c)], axis=1))
-    wc, wab = w[:, :PART], w[:, PART:]
+    core_id = core.reshape(1).astype(jnp.int32)
+    mine, theirs = split(core_id, qkv_weight)
+    wc, wab = merge(core_id, mine, shift(theirs, "core", NC, 1))
     other = shift(own, "core", NC, 1)
 
     seg = segments[0]
@@ -273,17 +300,11 @@
     one_hot = (owner[:, None] == jnp.arange(DEV, dtype=jnp.int32)[None, :]).astype(jnp.int32)
     rank = jnp.sum(jnp.cumsum(one_hot, axis=0) * one_hot, axis=1) - 1
     slot = owner * CAP + rank
-    table = jnp.stack(
-        [positions(seg, prefix), seg, slot, target % TOK, jnp.broadcast_to(prefix, seg.shape)]
-    )
+    table = jnp.stack([positions(seg, prefix), seg, slot, jnp.broadcast_to(prefix, seg.shape)])
     tables = jnp.stack([table, shift(table, "core", NC, 1)])
-    pos, segs, slots, rows, prefixes = (tables[:, k] for k in range(5))
-    hit = slots[:, None, :] == jnp.arange(DEV * CAP, dtype=jnp.int32)[None, :, None]
-    send = jnp.sum(jnp.where(hit, rows[:, None, :], 0), axis=2).reshape(2, NCHIP, NC, CAP)
-    send = lax.dynamic_index_in_dim(send, core, 2, keepdims=False)
-    send = jnp.where(core == 0, send, send[::-1]).transpose(1, 0, 2).reshape(NCHIP, NC * CAP)
-    send = jnp.concatenate([send // 16, send % 16], axis=1).astype(bf16)
-    send = jnp.pad(send[:, None, :], ((0, 0), (0, 15), (0, PART - 2 * NC * CAP)))
+    pos, segs, slots, prefixes = (tables[:, k] for k in range(4))
+    hit = slot[None, :] == jnp.arange(DEV * CAP, dtype=jnp.int32)[:, None]
+    send_places = jnp.sum(jnp.where(hit, (target % TOK)[None, :], 0), axis=1)
     frequency = ROPE_BASE ** (
         -2.0 * jnp.arange(HEAD_DIM // 2, dtype=f32) / HEAD_DIM
     )
@@ -299,20 +320,23 @@
     lanes = (zi - jnp.array(OFFSETS_C, jnp.int32)) % NZ * (D // NZ)
 
     tie = lax.optimization_barrier
-    up, down = shift(wab, "dp", NZ, 1), shift(wab, "dp", NZ, -1)
-    up, down, wc = tie((up, down, wc))
-    up3 = shift(jnp.stack([wab, up, down]), "dp", NZ, 3)
-    down3 = shift(jnp.stack([wab, up]), "dp", NZ, -3)
-    wz = assemble(z_ab, wab, up, down, up3, down3)
+    c0 = lax.all_to_all(wc, chips, split_axis=0, concat_axis=0, tiled=True)
+    c0 = c0.reshape(D // NZ, PART)
+    up = shift(wab, "dp", NZ, 1)
+    down = shift(wab, "dp", NZ, -1)
+    far = shift(wab, "dp", NZ, 4)
+    up2 = shift(jnp.stack([wab, up]), "dp", NZ, 2)
+    down2 = shift(jnp.stack([wab, down]), "dp", NZ, -2)
+    wz = assemble(z_ab, wab, up, down, far, up2, down2)
     wq = lax.all_gather(wz.reshape(NZ * 32, 2 * PART), chips, axis=0, tiled=True)
 
-    first = jnp.concatenate([jnp.broadcast_to(wc[None], (NCHIP, *wc.shape)), send], axis=1)
-    first = lax.all_to_all(first, chips, split_axis=0, concat_axis=0, tiled=True)
-    c0 = first[:, :32].reshape(D // NZ, PART)
-    places = first[:, 32, : 2 * NC * CAP].astype(jnp.int32)
-    places = (places[:, : NC * CAP] * 16 + places[:, NC * CAP :]).reshape(1, DEV * CAP)
-    c1 = each([c0, c0], "dp", NZ)
+    c1 = [shift(c0, "dp", NZ, 1)]
+    c1.append(shift(c0, "dp", NZ, -1))
+    places = lax.all_to_all(
+        send_places.reshape(DEV, CAP), plane, split_axis=0, concat_axis=0, tiled=True
+    ).reshape(1, DEV * CAP)
     c2 = each(c1, "dp", NZ)
+    c2, places = tie((c2, places))
     c3 = each(c2, "dp", NZ)
     c4 = each([c3[0][:, :HALF], c3[1][:, HALF:]], "dp", NZ)
     cur = project_kv(lanes, own, other, c0, *c1, *c2, *c3, *c4, cosine, sine)
@@ -322,16 +346,15 @@
         prev.append(lax.ppermute(cur[h], chips, onward))
     wq = wq.reshape(NCHIP, NZ, 32, 2 * PART)
 
-    got = []
+    whole = []
     for head in range(2):
         q = project_q(head, own, other, wq, cosine, sine)
         packed = attend(q, cur[head], prev[head], info, segc, segr, slots)
-        got.append(
-            lax.all_to_all(
-                packed.reshape(DEV, NC * CAP, PART), plane, split_axis=0, concat_axis=0, tiled=True
-            ).reshape(NCHIP, NC, NC * CAP, PART)
-        )
-    return place(places, got[0], got[1])[None]
+        got = lax.all_to_all(
+            packed.reshape(DEV, NC * CAP, PART), plane, split_axis=0, concat_axis=0, tiled=True
+        ).reshape(NCHIP, NC, NC * CAP, PART)
+        whole = [place(places, got, head, whole)]
+    return whole[0][None]
 
 
 def solution(mesh):

time: 244 us -> 234 us (0.959)
  blocking collectives: 24.8 us -> 18 us
  waiting for transfers between devices: 76.1 us -> 70.7 us
  Pallas kernels: 50.6 us -> 55.8 us
  starting transfers between devices: 55.7 us -> 53.1 us
    ppermute x15 -> x16, waiting for transfers between devices: 41.4 us -> 30 us  [shift(): return lax.ppermute(x, axis, [(i, (i + d) % n) for i in range(n)])]
    all_to_all x0 -> x1, waiting for transfers between devices: none -> 7.51 us  [on_device(): c0 = lax.all_to_all(wc, chips, split_axis=0, concat_axis=0, tiled=True)]
    all_to_all x0 -> x1, starting transfers between devices: none -> 6.81 us  [on_device(): c0 = lax.all_to_all(wc, chips, split_axis=0, concat_axis=0, tiled=True)]
    all_to_all x1, blocking collectives: 24.8 us -> 18 us  [on_device(): lax.all_to_all(send_places.reshape(DEV, CAP), plane, split_axis=0, concat...]
    ppermute x15 -> x16, starting transfers between devices: 28.2 us -> 23.7 us  [shift(): return lax.ppermute(x, axis, [(i, (i + d) % n) for i in range(n)])]
    all_to_all x2, starting transfers between devices: 20.2 us -> 16.8 us  [on_device(): lax.all_to_all(packed.reshape(DEV, NC * CAP, PART), plane, split_axis=0,...]
    pallas_call x0 -> x2, Pallas kernels: none -> 3.23 us  [small_call(): pl.pallas_call(kernel, out_shape=[jax.ShapeDtypeStruct(x, bf16) for x in...]
    pallas_call x1 -> x2, Pallas kernels: 3.93 us -> 5.93 us  [place(): pl.pallas_call(place_kernel, out_shape=jax.ShapeDtypeStruct((TOK, HEADS *...]
  transfers between devices with their start and end apart: 20 -> 22, of which waited for: 12 -> 11; matrix products, arithmetic and copies ran while one was open for 5% -> 6% of each run, Pallas kernels for 14% -> 16%
where the time goes in v1:
time: 234 us; the launch traced here: 233 us
  waiting for transfers between devices  70.7 us (30%)
  Pallas kernels  55.8 us (24%)
  starting transfers between devices  53.1 us (23%)
  blocking collectives  18 us (8%)
  between operations  14.3 us (6%)
  local copies, waits for them, and re-layouts  10.9 us (5%)
  other arithmetic  10.5 us (4%)
    ppermute x16, waiting for transfers between devices, shift(): return lax.ppermute(x, axis, [(i, (i + d) % n) for i in range(n)])  30 us
    ppermute x16, starting transfers between devices, shift(): return lax.ppermute(x, axis, [(i, (i + d) % n) for i in range(n)])  23.7 us
    all_to_all x2, waiting for transfers between devices, on_device(): lax.all_to_all(packed.reshape(DEV, NC * CAP, PART), plane, split_axis=0,...  19.7 us
    pallas_call x2, Pallas kernels, attend(): pl.pallas_call(attend_kernel, out_shape=jax.ShapeDtypeStruct((DEV, 2, CAP...  19.4 us
    all_to_all x1, blocking collectives, on_device(): lax.all_to_all(send_places.reshape(DEV, CAP), plane, split_axis=0, concat...  18 us
    pallas_call x2, Pallas kernels, project_q(): pl.pallas_call(project_q_kernel, out_shape=jax.ShapeDtypeStruct((2, TOK,...  16.8 us
    all_to_all x2, starting transfers between devices, on_device(): lax.all_to_all(packed.reshape(DEV, NC * CAP, PART), plane, split_axis=0,...  16.8 us
    ppermute x2, waiting for transfers between devices, on_device(): prev.append(lax.ppermute(cur[h], chips, onward))  13.5 us
  transfers between devices with their start and end apart: 22, of which 11 were waited for; matrix products, arithmetic and copies ran while one was open for 6% of the time, Pallas kernels for 16%

profile of v1, /device:TPU:1, one launch (start us, length us, event | category | flops | bytes accessed | tf_op | source)
XLA Modules:
  0.0 233.3 jit_solution(6394899639771410121)
XLA Ops:
  8.1 3.2 %collective-permute-start = (bf16[16,1536]{1,0:T(8,128)(2,1)}, bf16[16,1536]{1,0:T(8,128)(2,1)S(1)}, u32[]{:S(2)}, u32[]{:S(2)}) collective-permute-start(bf16[16,1536]{1,0:T(8,128)(2,1)} %get-tuple-element.15), channel_id=1, source_target_pairs={{0,1},{1,0},{2,3},{3,2},{4,5},{5,4},{6,7},{7,6},{8,9},{9,8},{10,11... | collective-permute-start | bytes 147464 | tf_op jit(solution)/shard_map/ppermute | solution.py:31
  14.7 3.9 %collective-permute-start.8 = (bf16[32,1024]{1,0:T(8,128)(2,1)}, bf16[32,1024]{1,0:T(8,128)(2,1)S(1)}, u32[]{:S(2)}, u32[]{:S(2)}) collective-permute-start(bf16[32,1024]{1,0:T(8,128)(2,1)} %get-tuple-element.18.one_ref), channel_id=1, source_target_pairs={{0,224},{32,0},{64,32},{96,64},{128,96},{160,128},{192,160},{224,1... | collective-permute-start | bytes 196616 | tf_op jit(solution)/shard_map/ppermute | solution.py:31
  18.6 2.8 %collective-permute-start.9 = (bf16[32,1024]{1,0:T(8,128)(2,1)}, bf16[32,1024]{1,0:T(8,128)(2,1)S(1)}, u32[]{:S(2)}, u32[]{:S(2)}) collective-permute-start(bf16[32,1024]{1,0:T(8,128)(2,1)} %get-tuple-element.18.one_ref), channel_id=1, source_target_pairs={{0,128},{32,160},{64,192},{96,224},{128,0},{160,32},{192,64},{224,... | collective-permute-start | bytes 196616 | tf_op jit(solution)/shard_map/ppermute | solution.py:31
  21.4 3.6 %collective-permute-done.7.up_ref = bf16[32,1024]{1,0:T(8,128)(2,1)S(1)} collective-permute-done((bf16[32,1024]{1,0:T(8,128)(2,1)}, bf16[32,1024]{1,0:T(8,128)(2,1)S(1)}, u32[]{:S(2)}, u32[]{:S(2)}) %collective-permute-start.7) | collective-permute-done | bytes 65568 | tf_op jit(solution)/shard_map/ppermute | solution.py:31
  29.6 3.5 %collective-permute-done.11.down2_ref = bf16[2,32,1024]{2,1,0:T(8,128)(2,1)S(1)} collective-permute-done((bf16[2,32,1024]{2,1,0:T(8,128)(2,1)S(1)}, bf16[2,32,1024]{2,1,0:T(8,128)(2,1)S(1)}, u32[]{:S(2)}, u32[]{:S(2)}) %collective-permute-start.11) | collective-permute-done | bytes 131104 | tf_op jit(solution)/shard_map/ppermute | solution.py:31
  39.6 6.8 %all-to-all-start = ((bf16[16,32,512]{2,1,0:T(8,128)(2,1)}), bf16[16,32,512]{2,1,0:T(8,128)(2,1)}, u32[]{:S(2)}, u32[]{:S(2)}) async-start(bf16[16,32,512]{2,1,0:T(8,128)(2,1)} %get-tuple-element.16), calls=%async_computation | async-start | bytes 1048576 | tf_op jit(solution)/shard_map/all_to_all | solution.py:323
  49.3 7.5 %all-to-all-done = bf16[16,32,512]{2,1,0:T(8,128)(2,1)} async-done(((bf16[16,32,512]{2,1,0:T(8,128)(2,1)}), bf16[16,32,512]{2,1,0:T(8,128)(2,1)}, u32[]{:S(2)}, u32[]{:S(2)}) %all-to-all-start) | async-done | bytes 524320 | tf_op jit(solution)/shard_map/all_to_all | solution.py:323
  58.5 8.6 %collective-permute-done.3.refs_2_ = bf16[512,512]{1,0:T(8,128)(2,1)} collective-permute-done((bf16[512,512]{1,0:T(8,128)(2,1)}, bf16[512,512]{1,0:T(8,128)(2,1)}, u32[]{:S(2)}, u32[]{:S(2)}) %collective-permute-start.3) | collective-permute-done | bytes 524320 | tf_op jit(solution)/shard_map/ppermute | solution.py:31
  69.5 18.0 %all_to_all.24 = s32[32,1,24]{2,1,0:T(1,128)S(1)} all-to-all(s32[32,1,24]{2,1,0:T(1,128)S(1)} %bitcast.73), channel_id=1, replica_groups=mesh['dp'=8,'x'=4,'y'=4,'core'=2] {'x','y','core'}, dimensions={0} | all-to-all | bytes 6144 | tf_op jit(solution)/shard_map/all_to_all | solution.py:335
  89.5 2.7 %collective-permute-start.13 = (bf16[512,512]{1,0:T(8,128)(2,1)}, bf16[512,512]{1,0:T(8,128)(2,1)S(1)}, u32[]{:S(2)}, u32[]{:S(2)}) collective-permute-start(bf16[512,512]{1,0:T(8,128)(2,1)} %collective-permute-done.4.refs_4_), channel_id=1, source_target_pairs={{0,224},{32,0},{64,32},{96,64},{128,96},{160,128},{192,160},{224,1... | collective-permute-start | bytes 1572872 | tf_op jit(solution)/shard_map/ppermute | solution.py:31
  94.9 9.1 %collective-permute-done.12.refs_5_ = bf16[512,512]{1,0:T(8,128)(2,1)S(1)} collective-permute-done((bf16[512,512]{1,0:T(8,128)(2,1)}, bf16[512,512]{1,0:T(8,128)(2,1)S(1)}, u32[]{:S(2)}, u32[]{:S(2)}) %collective-permute-start.12) | collective-permute-done | bytes 524320 | tf_op jit(solution)/shard_map/ppermute | solution.py:31
  104.3 2.7 %collective-permute-start.15 = (bf16[512,256]{1,0:T(8,128)(2,1)S(1)}, bf16[512,256]{1,0:T(8,128)(2,1)}, u32[]{:S(2)}, u32[]{:S(2)}) collective-permute-start(bf16[512,256]{1,0:T(8,128)(2,1)S(1)} %slice.67), channel_id=1, source_target_pairs={{0,224},{32,0},{64,32},{96,64},{128,96},{160,128},{192,160},{224,1... | collective-permute-start | bytes 786440 | tf_op jit(solution)/shard_map/ppermute | solution.py:31
  114.5 8.5 %project_kv.1 = (bf16[2,384,256]{2,1,0:T(8,128)(2,1)}, bf16[2,384,256]{2,1,0:T(8,128)(2,1)}) custom-call(s32[8]{0:T(128)} %fusion.14.lane_ref, bf16[384,4096]{1,0:T(8,128)(2,1)} %bitcast.62, bf16[384,4096]{1,0:T(8,128)(2,1)} %copy-done, bf16[512,512]{1,0:T(8,128)(2,1)} %bitcast.1.refs_0_, bf16[512,512]{1,0:T(8,128)(2,1)} %collective-permute-done.1.refs_1_, ...), custom_call_target="tpu_custom_call" | custom-call | flops 1048576 | bytes 1048576 | tf_op jit(solution)/shard_map/project_kv/pallas_call | solution.py:139
  126.9 8.3 %project_q.3.q_ref = bf16[2,384,512]{2,1,0:T(8,128)(2,1)} custom-call(bf16[384,4096]{1,0:T(8,128)(2,1)} %bitcast.63, bf16[384,4096]{1,0:T(8,128)(2,1)} %copy-done, bf16[16,8,32,1024]{3,2,1,0:T(8,128)(2,1)} %bitcast.59, f32[2,384,128]{2,1,0:T(8,128)} %pad_maximum_fusion.cos_ref.refs_9_, f32[2,384,128]{2,1,0:T(8,128)} %pad_maximum_fusion.1.sin_ref.refs_10_), custom_call_target="tpu_custom_call" | custom-call | flops 1048576 | bytes 1048576 | tf_op jit(solution)/shard_map/project_q/pallas_call | solution.py:163
  136.0 9.7 %attend.3 = bf16[32,2,24,512]{3,2,1,0:T(8,128)(2,1)} custom-call(s32[3]{0:T(128)} %pad_add_fusion.2.info_ref, bf16[2,384,512]{2,1,0:T(8,128)(2,1)} %project_q.3.q_ref, bf16[2,384,256]{2,1,0:T(8,128)(2,1)} %get-tuple-element.22.cur_ref, bf16[2,384,256]{2,1,0:T(8,128)(2,1)} %copy-done.6, s32[2,384,1]{2,1,0:T(8,128)} %copy.20.segc_ref, ...), custom_call_target="tpu_custom_call" | custom-call | flops 1048576 | bytes 1048576 | tf_op jit(solution)/shard_map/attend/pallas_call | solution.py:233
  145.7 8.1 %all-to-all-start.3 = ((bf16[32,48,512]{2,1,0:T(8,128)(2,1)}), bf16[32,48,512]{2,1,0:T(8,128)(2,1)S(1)}, u32[]{:S(2)}, u32[]{:S(2)}) async-start(bf16[32,48,512]{2,1,0:T(8,128)(2,1)} %bitcast.66), calls=%async_computation.3 | async-start | bytes 3145728 | tf_op jit(solution)/shard_map/all_to_all | solution.py:353
  153.8 3.5 %collective-permute-start.16 = (bf16[2,384,256]{2,1,0:T(8,128)(2,1)S(1)}, bf16[2,384,256]{2,1,0:T(8,128)(2,1)S(1)}, u32[]{:S(2)}, u32[]{:S(2)}) collective-permute-start(bf16[2,384,256]{2,1,0:T(8,128)(2,1)S(1)} %copy-done.5), channel_id=1, source_target_pairs={{0,2},{2,4},{4,6},{6,8},{8,10},{10,12},{12,14},{14,16},{16,18},{18... | collective-permute-start | bytes 1179656 | tf_op jit(solution)/shard_map/ppermute | solution.py:346
  157.3 8.5 %project_q.2.q_ref = bf16[2,384,512]{2,1,0:T(8,128)(2,1)} custom-call(bf16[384,4096]{1,0:T(8,128)(2,1)} %bitcast.64, bf16[384,4096]{1,0:T(8,128)(2,1)} %copy-done, bf16[16,8,32,1024]{3,2,1,0:T(8,128)(2,1)} %bitcast.60, f32[2,384,128]{2,1,0:T(8,128)} %pad_maximum_fusion.cos_ref.refs_9_, f32[2,384,128]{2,1,0:T(8,128)} %pad_maximum_fusion.1.sin_ref.refs_10_), custom_call_target="tpu_custom_call" | custom-call | flops 1048576 | bytes 1048576 | tf_op jit(solution)/shard_map/project_q/pallas_call | solution.py:163
  165.8 13.5 %collective-permute-done.16.prev_ref = bf16[2,384,256]{2,1,0:T(8,128)(2,1)S(1)} collective-permute-done((bf16[2,384,256]{2,1,0:T(8,128)(2,1)S(1)}, bf16[2,384,256]{2,1,0:T(8,128)(2,1)S(1)}, u32[]{:S(2)}, u32[]{:S(2)}) %collective-permute-start.16) | collective-permute-done | bytes 393248 | tf_op jit(solution)/shard_map/ppermute | solution.py:346
  180.0 9.7 %attend.2 = bf16[32,2,24,512]{3,2,1,0:T(8,128)(2,1)} custom-call(s32[3]{0:T(128)} %pad_add_fusion.2.info_ref, bf16[2,384,512]{2,1,0:T(8,128)(2,1)} %project_q.2.q_ref, bf16[2,384,256]{2,1,0:T(8,128)(2,1)} %get-tuple-element.21.cur_ref, bf16[2,384,256]{2,1,0:T(8,128)(2,1)} %copy-done.7, s32[2,384,1]{2,1,0:T(8,128)} %copy.20.segc_ref, ...), custom_call_target="tpu_custom_call" | custom-call | flops 1048576 | bytes 1048576 | tf_op jit(solution)/shard_map/attend/pallas_call | solution.py:233
  190.9 8.7 %all-to-all-start.2 = ((bf16[32,48,512]{2,1,0:T(8,128)(2,1)}), bf16[32,48,512]{2,1,0:T(8,128)(2,1)S(1)}, u32[]{:S(2)}, u32[]{:S(2)}) async-start(bf16[32,48,512]{2,1,0:T(8,128)(2,1)} %bitcast.67), calls=%async_computation.2 | async-start | bytes 3145728 | tf_op jit(solution)/shard_map/all_to_all | solution.py:353
  199.7 3.0 %place.2.refs_0_ = bf16[384,2048]{1,0:T(8,128)(2,1)} custom-call(s32[1,768]{1,0:T(1,128)} %reshape.157.places_ref, bf16[16,2,48,512]{3,2,1,0:T(8,128)(2,1)} %bitcast.65), custom_call_target="tpu_custom_call" | custom-call | flops 1048576 | bytes 1048576 | tf_op jit(solution)/shard_map/place/pallas_call | solution.py:268
  202.6 19.7 %all-to-all-done.2 = bf16[32,48,512]{2,1,0:T(8,128)(2,1)S(1)} async-done(((bf16[32,48,512]{2,1,0:T(8,128)(2,1)}), bf16[32,48,512]{2,1,0:T(8,128)(2,1)S(1)}, u32[]{:S(2)}, u32[]{:S(2)}) %all-to-all-start.2) | async-done | bytes 1572896 | tf_op jit(solution)/shard_map/all_to_all | solution.py:353
  223.5 3.0 %place.3 = bf16[384,2048]{1,0:T(8,128)(2,1)} custom-call(s32[1,768]{1,0:T(1,128)} %reshape.157.places_ref, bf16[16,2,48,512]{3,2,1,0:T(8,128)(2,1)} %bitcast.68, bf16[384,2048]{1,0:T(8,128)(2,1)} %place.2.refs_0_), custom_call_target="tpu_custom_call", output_to_operand_aliasing={{}: (2, {})} | custom-call | flops 1048576 | bytes 1048576 | tf_op jit(solution)/shard_map/place/pallas_call | solution.py:268
  (111 shorter events, 42.4 us)
Async XLA Ops:
  6.5 32.9 %copy-start.16 = (s32[1,384]{1,0:T(1,128)S(1)}, s32[1,384]{1,0:T(1,128)}, u32[]{:S(2)}) copy-start(s32[1,384]{1,0:T(1,128)} %param.9) | copy-start | bytes 4612
  6.5 120.4 %all-gather.2.cloned.1.call-start = ((), (), s32[]{:S(2)}) async-start(), calls=%async_computation.4 | async-start | bytes 8912896 | tf_op jit(solution)/shard_map/all_gather | solution.py:331
  8.1 4.3 %collective-permute-start = (bf16[16,1536]{1,0:T(8,128)(2,1)}, bf16[16,1536]{1,0:T(8,128)(2,1)S(1)}, u32[]{:S(2)}, u32[]{:S(2)}) collective-permute-start(bf16[16,1536]{1,0:T(8,128)(2,1)} %get-tuple-element.15), channel_id=1, source_target_pairs={{0,1},{1,0},{2,3},{3,2},{4,5},{5,4},{6,7},{7,6},{8,9},{9,8},{10,11... | collective-permute-start | bytes 147464 | tf_op jit(solution)/shard_map/ppermute | solution.py:31
  14.7 6.7 %collective-permute-start.8 = (bf16[32,1024]{1,0:T(8,128)(2,1)}, bf16[32,1024]{1,0:T(8,128)(2,1)S(1)}, u32[]{:S(2)}, u32[]{:S(2)}) collective-permute-start(bf16[32,1024]{1,0:T(8,128)(2,1)} %get-tuple-element.18.one_ref), channel_id=1, source_target_pairs={{0,224},{32,0},{64,32},{96,64},{128,96},{160,128},{192,160},{224,1... | collective-permute-start | bytes 196616 | tf_op jit(solution)/shard_map/ppermute | solution.py:31
  18.6 6.4 %collective-permute-start.7 = (bf16[32,1024]{1,0:T(8,128)(2,1)}, bf16[32,1024]{1,0:T(8,128)(2,1)S(1)}, u32[]{:S(2)}, u32[]{:S(2)}) collective-permute-start(bf16[32,1024]{1,0:T(8,128)(2,1)} %get-tuple-element.18.one_ref), channel_id=1, source_target_pairs={{0,32},{32,64},{64,96},{96,128},{128,160},{160,192},{192,224},{224... | collective-permute-start | bytes 196616 | tf_op jit(solution)/shard_map/ppermute | solution.py:31
  18.6 11.0 %collective-permute-start.9 = (bf16[32,1024]{1,0:T(8,128)(2,1)}, bf16[32,1024]{1,0:T(8,128)(2,1)S(1)}, u32[]{:S(2)}, u32[]{:S(2)}) collective-permute-start(bf16[32,1024]{1,0:T(8,128)(2,1)} %get-tuple-element.18.one_ref), channel_id=1, source_target_pairs={{0,128},{32,160},{64,192},{96,224},{128,0},{160,32},{192,64},{224,... | collective-permute-start | bytes 196616 | tf_op jit(solution)/shard_map/ppermute | solution.py:31
  25.9 67.6 %copy-start.18 = (s32[8]{0:T(128)S(1)}, s32[8]{0:T(128)}, u32[]{:S(2)}) copy-start(s32[8]{0:T(128)} %constant.86) | copy-start | bytes 100
  25.9 7.2 %collective-permute-start.11 = (bf16[2,32,1024]{2,1,0:T(8,128)(2,1)S(1)}, bf16[2,32,1024]{2,1,0:T(8,128)(2,1)S(1)}, u32[]{:S(2)}, u32[]{:S(2)}) collective-permute-start(bf16[2,32,1024]{2,1,0:T(8,128)(2,1)S(1)} %get-tuple-element.27), channel_id=1, source_target_pairs={{0,192},{32,224},{64,0},{96,32},{128,64},{160,96},{192,128},{224,1... | collective-permute-start | bytes 393224 | tf_op jit(solution)/shard_map/ppermute | solution.py:31
  26.0 9.2 %collective-permute-start.10 = (bf16[2,32,1024]{2,1,0:T(8,128)(2,1)S(1)}, bf16[2,32,1024]{2,1,0:T(8,128)(2,1)S(1)}, u32[]{:S(2)}, u32[]{:S(2)}) collective-permute-start(bf16[2,32,1024]{2,1,0:T(8,128)(2,1)S(1)} %get-tuple-element.28), channel_id=1, source_target_pairs={{0,64},{32,96},{64,128},{96,160},{128,192},{160,224},{192,0},{224,... | collective-permute-start | bytes 393224 | tf_op jit(solution)/shard_map/ppermute | solution.py:31
  37.8 74.2 %collective-permute-start.6 = (bf16[384,4096]{1,0:T(8,128)(2,1)}, bf16[384,4096]{1,0:T(8,128)(2,1)S(1)}, u32[]{:S(2)}, u32[]{:S(2)}) collective-permute-start(bf16[384,4096]{1,0:T(8,128)(2,1)} %bitcast.61), channel_id=1, source_target_pairs={{0,1},{1,0},{2,3},{3,2},{4,5},{5,4},{6,7},{7,6},{8,9},{9,8},{10,11... | collective-permute-start | bytes 9437192 | tf_op jit(solution)/shard_map/ppermute | solution.py:31
  39.6 17.3 %all-to-all-start = ((bf16[16,32,512]{2,1,0:T(8,128)(2,1)}), bf16[16,32,512]{2,1,0:T(8,128)(2,1)}, u32[]{:S(2)}, u32[]{:S(2)}) async-start(bf16[16,32,512]{2,1,0:T(8,128)(2,1)} %get-tuple-element.16), calls=%async_computation | async-start | bytes 1048576 | tf_op jit(solution)/shard_map/all_to_all | solution.py:323
  56.9 10.3 %collective-permute-start.3 = (bf16[512,512]{1,0:T(8,128)(2,1)}, bf16[512,512]{1,0:T(8,128)(2,1)}, u32[]{:S(2)}, u32[]{:S(2)}) collective-permute-start(bf16[512,512]{1,0:T(8,128)(2,1)} %bitcast.1.refs_0_), channel_id=1, source_target_pairs={{0,224},{32,0},{64,32},{96,64},{128,96},{160,128},{192,160},{224,1... | collective-permute-start | bytes 1572872 | tf_op jit(solution)/shard_map/ppermute | solution.py:31
  56.9 11.7 %collective-permute-start.1 = (bf16[512,512]{1,0:T(8,128)(2,1)}, bf16[512,512]{1,0:T(8,128)(2,1)}, u32[]{:S(2)}, u32[]{:S(2)}) collective-permute-start(bf16[512,512]{1,0:T(8,128)(2,1)} %bitcast.1.refs_0_), channel_id=1, source_target_pairs={{0,32},{32,64},{64,96},{96,128},{128,160},{160,192},{192,224},{224... | collective-permute-start | bytes 1572872 | tf_op jit(solution)/shard_map/ppermute | solution.py:31
  67.1 22.4 %collective-permute-start.4 = (bf16[512,512]{1,0:T(8,128)(2,1)}, bf16[512,512]{1,0:T(8,128)(2,1)}, u32[]{:S(2)}, u32[]{:S(2)}) collective-permute-start(bf16[512,512]{1,0:T(8,128)(2,1)} %collective-permute-done.3.refs_2_), channel_id=1, source_target_pairs={{0,224},{32,0},{64,32},{96,64},{128,96},{160,128},{192,160},{224,1... | collective-permute-start | bytes 1572872 | tf_op jit(solution)/shard_map/ppermute | solution.py:31
  68.6 20.9 %collective-permute-start.2 = (bf16[512,512]{1,0:T(8,128)(2,1)}, bf16[512,512]{1,0:T(8,128)(2,1)}, u32[]{:S(2)}, u32[]{:S(2)}) collective-permute-start(bf16[512,512]{1,0:T(8,128)(2,1)} %collective-permute-done.1.refs_1_), channel_id=1, source_target_pairs={{0,32},{32,64},{64,96},{96,128},{128,160},{160,192},{192,224},{224... | collective-permute-start | bytes 1572872 | tf_op jit(solution)/shard_map/ppermute | solution.py:31
  89.5 14.4 %collective-permute-start.12 = (bf16[512,512]{1,0:T(8,128)(2,1)}, bf16[512,512]{1,0:T(8,128)(2,1)S(1)}, u32[]{:S(2)}, u32[]{:S(2)}) collective-permute-start(bf16[512,512]{1,0:T(8,128)(2,1)} %collective-permute-done.2.refs_3_), channel_id=1, source_target_pairs={{0,32},{32,64},{64,96},{96,128},{128,160},{160,192},{192,224},{224... | collective-permute-start | bytes 1572872 | tf_op jit(solution)/shard_map/ppermute | solution.py:31
  89.5 14.7 %collective-permute-start.13 = (bf16[512,512]{1,0:T(8,128)(2,1)}, bf16[512,512]{1,0:T(8,128)(2,1)S(1)}, u32[]{:S(2)}, u32[]{:S(2)}) collective-permute-start(bf16[512,512]{1,0:T(8,128)(2,1)} %collective-permute-done.4.refs_4_), channel_id=1, source_target_pairs={{0,224},{32,0},{64,32},{96,64},{128,96},{160,128},{192,160},{224,1... | collective-permute-start | bytes 1572872 | tf_op jit(solution)/shard_map/ppermute | solution.py:31
  92.2 2.1 collective-permute-start.5
  103.9 8.1 %collective-permute-start.14 = (bf16[512,256]{1,0:T(8,128)(2,1)S(1)}, bf16[512,256]{1,0:T(8,128)(2,1)S(1)}, u32[]{:S(2)}, u32[]{:S(2)}) collective-permute-start(bf16[512,256]{1,0:T(8,128)(2,1)S(1)} %slice.66), channel_id=1, source_target_pairs={{0,32},{32,64},{64,96},{96,128},{128,160},{160,192},{192,224},{224... | collective-permute-start | bytes 786440 | tf_op jit(solution)/shard_map/ppermute | solution.py:31
  104.3 7.8 %collective-permute-start.15 = (bf16[512,256]{1,0:T(8,128)(2,1)S(1)}, bf16[512,256]{1,0:T(8,128)(2,1)}, u32[]{:S(2)}, u32[]{:S(2)}) collective-permute-start(bf16[512,256]{1,0:T(8,128)(2,1)S(1)} %slice.67), channel_id=1, source_target_pairs={{0,224},{32,0},{64,32},{96,64},{128,96},{160,128},{192,160},{224,1... | collective-permute-start | bytes 786440 | tf_op jit(solution)/shard_map/ppermute | solution.py:31
  123.0 12.3 %collective-permute-start.17 = (bf16[2,384,256]{2,1,0:T(8,128)(2,1)}, bf16[2,384,256]{2,1,0:T(8,128)(2,1)S(1)}, u32[]{:S(2)}, u32[]{:S(2)}) collective-permute-start(bf16[2,384,256]{2,1,0:T(8,128)(2,1)} %get-tuple-element.22.cur_ref), channel_id=1, source_target_pairs={{0,2},{2,4},{4,6},{6,8},{8,10},{10,12},{12,14},{14,16},{16,18},{18... | collective-permute-start | bytes 1179656 | tf_op jit(solution)/shard_map/ppermute | solution.py:346
  145.7 44.1 %all-to-all-start.3 = ((bf16[32,48,512]{2,1,0:T(8,128)(2,1)}), bf16[32,48,512]{2,1,0:T(8,128)(2,1)S(1)}, u32[]{:S(2)}, u32[]{:S(2)}) async-start(bf16[32,48,512]{2,1,0:T(8,128)(2,1)} %bitcast.66), calls=%async_computation.3 | async-start | bytes 3145728 | tf_op jit(solution)/shard_map/all_to_all | solution.py:353
  153.8 25.5 %collective-permute-start.16 = (bf16[2,384,256]{2,1,0:T(8,128)(2,1)S(1)}, bf16[2,384,256]{2,1,0:T(8,128)(2,1)S(1)}, u32[]{:S(2)}, u32[]{:S(2)}) collective-permute-start(bf16[2,384,256]{2,1,0:T(8,128)(2,1)S(1)} %copy-done.5), channel_id=1, source_target_pairs={{0,2},{2,4},{4,6},{6,8},{8,10},{10,12},{12,14},{14,16},{16,18},{18... | collective-permute-start | bytes 1179656 | tf_op jit(solution)/shard_map/ppermute | solution.py:346
  190.9 31.4 %all-to-all-start.2 = ((bf16[32,48,512]{2,1,0:T(8,128)(2,1)}), bf16[32,48,512]{2,1,0:T(8,128)(2,1)S(1)}, u32[]{:S(2)}, u32[]{:S(2)}) async-start(bf16[32,48,512]{2,1,0:T(8,128)(2,1)} %bitcast.67), calls=%async_computation.2 | async-start | bytes 3145728 | tf_op jit(solution)/shard_map/all_to_all | solution.py:353
  (17 other events, 116.3 us)
Sparse Core Ops, SparseCore 0:
  37.9 74.5 all-gather.1

commit v2 on v1

--- a/solution.py
+++ b/solution.py
@@ -124,14 +124,16 @@
     depth = D // NZ
     for n in range(2):
         cols = slice(n * HALF, (n + 1) * HALF)
-        for b, ref in enumerate((own_ref, other_ref)):
-            acc = None
-            for k in range(NZ):
-                w = w_refs[k][:, cols] if k < NZ - 1 else w_refs[NZ - 1 + n][...]
-                tok = ref[:, pl.ds(pl.multiple_of(lane_ref[k], depth), depth)]
-                term = jnp.dot(tok, w, preferred_element_type=f32)
-                acc = term if acc is None else acc + term
-            finish(acc, 1, cos_ref, sin_ref, (first_ref, second_ref)[n], b)
+        acc = None
+        for k in range(NZ):
+            w = w_refs[k][:, cols] if k < NZ - 1 else w_refs[NZ - 1 + n][...]
+            at = pl.ds(pl.multiple_of(lane_ref[k], depth), depth)
+            tok = jnp.concatenate([own_ref[:, at], other_ref[:, at]])
+            term = jnp.dot(tok, w, preferred_element_type=f32)
+            acc = term if acc is None else acc + term
+        for b in range(2):
+            rows = acc[b * TOK : (b + 1) * TOK]
+            finish(rows, 1, cos_ref, sin_ref, (first_ref, second_ref)[n], b)
 
 
 def project_kv(lanes, *arrays):
@@ -148,13 +150,15 @@
 
 def project_q_kernel(own_ref, other_ref, w_ref, cos_ref, sin_ref, out_ref):
     depth = D // NZ
-    for b, ref in enumerate((own_ref, other_ref)):
-        acc = None
-        for z in range(NZ):
-            w = w_ref[:, z].reshape(depth, HALF)
-            term = jnp.dot(ref[:, z * depth : (z + 1) * depth], w, preferred_element_type=f32)
-            acc = term if acc is None else acc + term
-        finish(acc, 2, cos_ref, sin_ref, out_ref, b)
+    acc = None
+    for z in range(NZ):
+        w = w_ref[:, z].reshape(depth, HALF)
+        at = slice(z * depth, (z + 1) * depth)
+        tok = jnp.concatenate([own_ref[:, at], other_ref[:, at]])
+        term = jnp.dot(tok, w, preferred_element_type=f32)
+        acc = term if acc is None else acc + term
+    for b in range(2):
+        finish(acc[b * TOK : (b + 1) * TOK], 2, cos_ref, sin_ref, out_ref, b)
 
 
 def project_q(head, own, other, w, cosine, sine):
@@ -335,9 +339,11 @@
     places = lax.all_to_all(
         send_places.reshape(DEV, CAP), plane, split_axis=0, concat_axis=0, tiled=True
     ).reshape(1, DEV * CAP)
-    c2 = each(c1, "dp", NZ)
+    c2 = [shift(c1[0], "dp", NZ, 1)]
+    c2.append(shift(c1[1], "dp", NZ, -1))
     c2, places = tie((c2, places))
     c3 = each(c2, "dp", NZ)
+    c3, segc, segr, slots, info, cosine, sine = tie((c3, segc, segr, slots, info, cosine, sine))
     c4 = each([c3[0][:, :HALF], c3[1][:, HALF:]], "dp", NZ)
     cur = project_kv(lanes, own, other, c0, *c1, *c2, *c3, *c4, cosine, sine)
     onward = [(i, i + 1) for i in range(NCHIP - 1)]

time: 234 us -> 242 us (1.034)
  blocking collectives: 18 us -> 0 us
  waiting for transfers between devices: 70.7 us -> 88.6 us
  starting transfers between devices: 53.1 us -> 61.4 us
    all_to_all x1 -> x0, blocking collectives: 18 us -> none  [on_device(): lax.all_to_all(send_places.reshape(DEV, CAP), plane, split_axis=0, concat...]
    all_to_all x0 -> x1, starting transfers between devices: none -> 8.97 us  [on_device(): lax.all_to_all(send_places.reshape(DEV, CAP), plane, split_axis=0, concat...]
    all_to_all x0 -> x1, waiting for transfers between devices: none -> 6.82 us  [on_device(): lax.all_to_all(send_places.reshape(DEV, CAP), plane, split_axis=0, concat...]
    all_to_all x1, waiting for transfers between devices: 7.51 us -> 14 us  [on_device(): c0 = lax.all_to_all(wc, chips, split_axis=0, concat_axis=0, tiled=True)]
    ppermute x16, waiting for transfers between devices: 30 us -> 34.4 us  [shift(): return lax.ppermute(x, axis, [(i, (i + d) % n) for i in range(n)])]
    unnamed x40 -> x42, local copies, waits for them, and re-layouts: 7.56 us -> 7.56 us
  transfers between devices with their start and end apart: 22 -> 23, of which waited for: 11 -> 12; matrix products, arithmetic and copies ran while one was open for 6% -> 6% of each run, Pallas kernels for 16% -> 16%
where the time goes in v2:
time: 242 us
  waiting for transfers between devices  88.6 us (37%)
  starting transfers between devices  61.4 us (25%)
  Pallas kernels  55.5 us (23%)
  between operations  14.3 us (6%)
  local copies, waits for them, and re-layouts  11.5 us (5%)
  other arithmetic  10.3 us (4%)
    ppermute x16, waiting for transfers between devices, shift(): return lax.ppermute(x, axis, [(i, (i + d) % n) for i in range(n)])  34.4 us
    ppermute x16, starting transfers between devices, shift(): return lax.ppermute(x, axis, [(i, (i + d) % n) for i in range(n)])  22.4 us
    all_to_all x2, waiting for transfers between devices, on_device(): lax.all_to_all(packed.reshape(DEV, NC * CAP, PART), plane, split_axis=0,...  19.7 us
    pallas_call x2, Pallas kernels, attend(): pl.pallas_call(attend_kernel, out_shape=jax.ShapeDtypeStruct((DEV, 2, CAP...  19.4 us
    all_to_all x2, starting transfers between devices, on_device(): lax.all_to_all(packed.reshape(DEV, NC * CAP, PART), plane, split_axis=0,...  17.5 us
    pallas_call x2, Pallas kernels, project_q(): pl.pallas_call(project_q_kernel, out_shape=jax.ShapeDtypeStruct((2, TOK,...  16.4 us
    all_to_all x1, waiting for transfers between devices, on_device(): c0 = lax.all_to_all(wc, chips, split_axis=0, concat_axis=0, tiled=True)  14 us
    ppermute x2, waiting for transfers between devices, on_device(): prev.append(lax.ppermute(cur[h], chips, onward))  13.7 us
  transfers between devices with their start and end apart: 23, of which 12 were waited for; matrix products, arithmetic and copies ran while one was open for 6% of the time, Pallas kernels for 16%

profile of v2, /device:TPU:1, one launch (start us, length us, event | category | flops | bytes accessed | tf_op | source)
XLA Modules:
  0.0 241.6 jit_solution(6342368114802036273)
XLA Ops:
  8.1 3.2 %collective-permute-start = (bf16[16,1536]{1,0:T(8,128)(2,1)}, bf16[16,1536]{1,0:T(8,128)(2,1)S(1)}, u32[]{:S(2)}, u32[]{:S(2)}) collective-permute-start(bf16[16,1536]{1,0:T(8,128)(2,1)} %get-tuple-element.23), channel_id=1, source_target_pairs={{0,1},{1,0},{2,3},{3,2},{4,5},{5,4},{6,7},{7,6},{8,9},{9,8},{10,11... | collective-permute-start | bytes 147464 | tf_op jit(solution)/shard_map/ppermute | solution.py:31
  14.7 3.9 %collective-permute-start.10 = (bf16[32,1024]{1,0:T(8,128)(2,1)}, bf16[32,1024]{1,0:T(8,128)(2,1)S(1)}, u32[]{:S(2)}, u32[]{:S(2)}) collective-permute-start(bf16[32,1024]{1,0:T(8,128)(2,1)} %get-tuple-element.29.one_ref), channel_id=1, source_target_pairs={{0,224},{32,0},{64,32},{96,64},{128,96},{160,128},{192,160},{224,1... | collective-permute-start | bytes 196616 | tf_op jit(solution)/shard_map/ppermute | solution.py:31
  21.3 3.6 %collective-permute-done.9.up_ref = bf16[32,1024]{1,0:T(8,128)(2,1)S(1)} collective-permute-done((bf16[32,1024]{1,0:T(8,128)(2,1)}, bf16[32,1024]{1,0:T(8,128)(2,1)S(1)}, u32[]{:S(2)}, u32[]{:S(2)}) %collective-permute-start.9) | collective-permute-done | bytes 65568 | tf_op jit(solution)/shard_map/ppermute | solution.py:31
  29.5 3.6 %collective-permute-done.13.down2_ref = bf16[2,32,1024]{2,1,0:T(8,128)(2,1)S(1)} collective-permute-done((bf16[2,32,1024]{2,1,0:T(8,128)(2,1)S(1)}, bf16[2,32,1024]{2,1,0:T(8,128)(2,1)S(1)}, u32[]{:S(2)}, u32[]{:S(2)}) %collective-permute-start.13) | collective-permute-done | bytes 131104 | tf_op jit(solution)/shard_map/ppermute | solution.py:31
  42.4 6.8 %all-to-all-start = ((bf16[16,32,512]{2,1,0:T(8,128)(2,1)}), bf16[16,32,512]{2,1,0:T(8,128)(2,1)}, u32[]{:S(2)}, u32[]{:S(2)}) async-start(bf16[16,32,512]{2,1,0:T(8,128)(2,1)} %get-tuple-element.24), calls=%async_computation | async-start | bytes 1048576 | tf_op jit(solution)/shard_map/all_to_all | solution.py:327
  49.3 14.0 %all-to-all-done = bf16[16,32,512]{2,1,0:T(8,128)(2,1)} async-done(((bf16[16,32,512]{2,1,0:T(8,128)(2,1)}), bf16[16,32,512]{2,1,0:T(8,128)(2,1)}, u32[]{:S(2)}, u32[]{:S(2)}) %all-to-all-start) | async-done | bytes 524320 | tf_op jit(solution)/shard_map/all_to_all | solution.py:327
  65.5 9.6 %collective-permute-done.3.refs_2_ = bf16[512,512]{1,0:T(8,128)(2,1)} collective-permute-done((bf16[512,512]{1,0:T(8,128)(2,1)}, bf16[512,512]{1,0:T(8,128)(2,1)}, u32[]{:S(2)}, u32[]{:S(2)}) %collective-permute-start.3) | collective-permute-done | bytes 524320 | tf_op jit(solution)/shard_map/ppermute | solution.py:31
  77.6 9.0 %all-to-all-start.1 = ((s32[32,1,24]{2,1,0:T(1,128)}), s32[32,1,24]{2,1,0:T(1,128)S(1)}, u32[]{:S(2)}, u32[]{:S(2)}) async-start(s32[32,1,24]{2,1,0:T(1,128)} %bitcast.3), calls=%async_computation.1 | async-start | bytes 32768 | tf_op jit(solution)/shard_map/all_to_all | solution.py:339
  86.9 6.8 %all-to-all-done.1 = s32[32,1,24]{2,1,0:T(1,128)S(1)} async-done(((s32[32,1,24]{2,1,0:T(1,128)}), s32[32,1,24]{2,1,0:T(1,128)S(1)}, u32[]{:S(2)}, u32[]{:S(2)}) %all-to-all-start.1) | async-done | bytes 3104 | tf_op jit(solution)/shard_map/all_to_all | solution.py:339
  103.1 7.8 %collective-permute-done.5.refs_5_ = bf16[512,512]{1,0:T(8,128)(2,1)S(1)} collective-permute-done((bf16[512,512]{1,0:T(8,128)(2,1)}, bf16[512,512]{1,0:T(8,128)(2,1)S(1)}, u32[]{:S(2)}, u32[]{:S(2)}) %collective-permute-start.5) | collective-permute-done | bytes 524320 | tf_op jit(solution)/shard_map/ppermute | solution.py:31
  114.0 3.5 %collective-permute-done.15.refs_8_ = bf16[512,256]{1,0:T(8,128)(2,1)S(1)} collective-permute-done((bf16[512,256]{1,0:T(8,128)(2,1)S(1)}, bf16[512,256]{1,0:T(8,128)(2,1)S(1)}, u32[]{:S(2)}, u32[]{:S(2)}) %collective-permute-start.15) | collective-permute-done | bytes 262176 | tf_op jit(solution)/shard_map/ppermute | solution.py:31
  117.5 3.1 %collective-permute-done.14.refs_7_ = bf16[512,256]{1,0:T(8,128)(2,1)S(1)} collective-permute-done((bf16[512,256]{1,0:T(8,128)(2,1)S(1)}, bf16[512,256]{1,0:T(8,128)(2,1)S(1)}, u32[]{:S(2)}, u32[]{:S(2)}) %collective-permute-start.14) | collective-permute-done | bytes 262176 | tf_op jit(solution)/shard_map/ppermute | solution.py:31
  123.0 8.6 %project_kv.1 = (bf16[2,384,256]{2,1,0:T(8,128)(2,1)}, bf16[2,384,256]{2,1,0:T(8,128)(2,1)}) custom-call(s32[8]{0:T(128)} %fusion.14.lane_ref, bf16[384,4096]{1,0:T(8,128)(2,1)} %bitcast.62, bf16[384,4096]{1,0:T(8,128)(2,1)} %copy-done, bf16[512,512]{1,0:T(8,128)(2,1)} %bitcast.1.refs_0_, bf16[512,512]{1,0:T(8,128)(2,1)} %collective-permute-done.1.refs_1_, ...), custom_call_target="tpu_custom_call" | custom-call | flops 1048576 | bytes 1048576 | tf_op jit(solution)/shard_map/project_kv/pallas_call | solution.py:141
  134.7 8.1 %project_q.3.q_ref = bf16[2,384,512]{2,1,0:T(8,128)(2,1)} custom-call(bf16[384,4096]{1,0:T(8,128)(2,1)} %bitcast.63, bf16[384,4096]{1,0:T(8,128)(2,1)} %copy-done, bf16[16,8,32,1024]{3,2,1,0:T(8,128)(2,1)} %bitcast.59, f32[2,384,128]{2,1,0:T(8,128)} %pad_maximum_fusion.cos_ref.refs_9_, f32[2,384,128]{2,1,0:T(8,128)} %pad_maximum_fusion.1.sin_ref.refs_10_), custom_call_target="tpu_custom_call" | custom-call | flops 1048576 | bytes 1048576 | tf_op jit(solution)/shard_map/project_q/pallas_call | solution.py:167
  143.6 9.7 %attend.3 = bf16[32,2,24,512]{3,2,1,0:T(8,128)(2,1)} custom-call(s32[3]{0:T(128)} %pad_add_fusion.2.info_ref, bf16[2,384,512]{2,1,0:T(8,128)(2,1)} %project_q.3.q_ref, bf16[2,384,256]{2,1,0:T(8,128)(2,1)} %get-tuple-element.38.cur_ref, bf16[2,384,256]{2,1,0:T(8,128)(2,1)} %copy-done.7, s32[2,384,1]{2,1,0:T(8,128)} %copy.20.segc_ref, ...), custom_call_target="tpu_custom_call" | custom-call | flops 1048576 | bytes 1048576 | tf_op jit(solution)/shard_map/attend/pallas_call | solution.py:237
  153.3 8.7 %all-to-all-start.3 = ((bf16[32,48,512]{2,1,0:T(8,128)(2,1)}), bf16[32,48,512]{2,1,0:T(8,128)(2,1)S(1)}, u32[]{:S(2)}, u32[]{:S(2)}) async-start(bf16[32,48,512]{2,1,0:T(8,128)(2,1)} %bitcast.66), calls=%async_computation.3 | async-start | bytes 3145728 | tf_op jit(solution)/shard_map/all_to_all | solution.py:359
  162.0 3.5 %collective-permute-start.16 = (bf16[2,384,256]{2,1,0:T(8,128)(2,1)S(1)}, bf16[2,384,256]{2,1,0:T(8,128)(2,1)S(1)}, u32[]{:S(2)}, u32[]{:S(2)}) collective-permute-start(bf16[2,384,256]{2,1,0:T(8,128)(2,1)S(1)} %copy-done.5), channel_id=1, source_target_pairs={{0,2},{2,4},{4,6},{6,8},{8,10},{10,12},{12,14},{14,16},{16,18},{18... | collective-permute-start | bytes 1179656 | tf_op jit(solution)/shard_map/ppermute | solution.py:352
  165.6 8.3 %project_q.2.q_ref = bf16[2,384,512]{2,1,0:T(8,128)(2,1)} custom-call(bf16[384,4096]{1,0:T(8,128)(2,1)} %bitcast.64, bf16[384,4096]{1,0:T(8,128)(2,1)} %copy-done, bf16[16,8,32,1024]{3,2,1,0:T(8,128)(2,1)} %bitcast.60, f32[2,384,128]{2,1,0:T(8,128)} %pad_maximum_fusion.cos_ref.refs_9_, f32[2,384,128]{2,1,0:T(8,128)} %pad_maximum_fusion.1.sin_ref.refs_10_), custom_call_target="tpu_custom_call" | custom-call | flops 1048576 | bytes 1048576 | tf_op jit(solution)/shard_map/project_q/pallas_call | solution.py:167
  173.8 13.7 %collective-permute-done.16.prev_ref = bf16[2,384,256]{2,1,0:T(8,128)(2,1)S(1)} collective-permute-done((bf16[2,384,256]{2,1,0:T(8,128)(2,1)S(1)}, bf16[2,384,256]{2,1,0:T(8,128)(2,1)S(1)}, u32[]{:S(2)}, u32[]{:S(2)}) %collective-permute-start.16) | collective-permute-done | bytes 393248 | tf_op jit(solution)/shard_map/ppermute | solution.py:352
  188.3 9.7 %attend.2 = bf16[32,2,24,512]{3,2,1,0:T(8,128)(2,1)} custom-call(s32[3]{0:T(128)} %pad_add_fusion.2.info_ref, bf16[2,384,512]{2,1,0:T(8,128)(2,1)} %project_q.2.q_ref, bf16[2,384,256]{2,1,0:T(8,128)(2,1)} %get-tuple-element.34.cur_ref, bf16[2,384,256]{2,1,0:T(8,128)(2,1)} %copy-done.6, s32[2,384,1]{2,1,0:T(8,128)} %copy.20.segc_ref, ...), custom_call_target="tpu_custom_call" | custom-call | flops 1048576 | bytes 1048576 | tf_op jit(solution)/shard_map/attend/pallas_call | solution.py:237
  199.2 8.8 %all-to-all-start.2 = ((bf16[32,48,512]{2,1,0:T(8,128)(2,1)}), bf16[32,48,512]{2,1,0:T(8,128)(2,1)S(1)}, u32[]{:S(2)}, u32[]{:S(2)}) async-start(bf16[32,48,512]{2,1,0:T(8,128)(2,1)} %bitcast.67), calls=%async_computation.2 | async-start | bytes 3145728 | tf_op jit(solution)/shard_map/all_to_all | solution.py:359
  208.0 3.0 %place.2.refs_0_ = bf16[384,2048]{1,0:T(8,128)(2,1)} custom-call(s32[1,768]{1,0:T(1,128)} %reshape.157.places_ref, bf16[16,2,48,512]{3,2,1,0:T(8,128)(2,1)} %bitcast.65), custom_call_target="tpu_custom_call" | custom-call | flops 1048576 | bytes 1048576 | tf_op jit(solution)/shard_map/place/pallas_call | solution.py:272
  210.9 19.7 %all-to-all-done.2 = bf16[32,48,512]{2,1,0:T(8,128)(2,1)S(1)} async-done(((bf16[32,48,512]{2,1,0:T(8,128)(2,1)}), bf16[32,48,512]{2,1,0:T(8,128)(2,1)S(1)}, u32[]{:S(2)}, u32[]{:S(2)}) %all-to-all-start.2) | async-done | bytes 1572896 | tf_op jit(solution)/shard_map/all_to_all | solution.py:359
  231.8 3.0 %place.3 = bf16[384,2048]{1,0:T(8,128)(2,1)} custom-call(s32[1,768]{1,0:T(1,128)} %reshape.157.places_ref, bf16[16,2,48,512]{3,2,1,0:T(8,128)(2,1)} %bitcast.68, bf16[384,2048]{1,0:T(8,128)(2,1)} %place.2.refs_0_), custom_call_target="tpu_custom_call", output_to_operand_aliasing={{}: (2, {})} | custom-call | flops 1048576 | bytes 1048576 | tf_op jit(solution)/shard_map/place/pallas_call | solution.py:272
  (114 shorter events, 47.8 us)
Async XLA Ops:
  6.5 128.2 %all-gather.2.cloned.1.call-start = ((), (), s32[]{:S(2)}) async-start(), calls=%async_computation.4 | async-start | bytes 8912896 | tf_op jit(solution)/shard_map/all_gather | solution.py:335
  8.1 4.3 %collective-permute-start = (bf16[16,1536]{1,0:T(8,128)(2,1)}, bf16[16,1536]{1,0:T(8,128)(2,1)S(1)}, u32[]{:S(2)}, u32[]{:S(2)}) collective-permute-start(bf16[16,1536]{1,0:T(8,128)(2,1)} %get-tuple-element.23), channel_id=1, source_target_pairs={{0,1},{1,0},{2,3},{3,2},{4,5},{5,4},{6,7},{7,6},{8,9},{9,8},{10,11... | collective-permute-start | bytes 147464 | tf_op jit(solution)/shard_map/ppermute | solution.py:31
  14.7 6.7 %collective-permute-start.10 = (bf16[32,1024]{1,0:T(8,128)(2,1)}, bf16[32,1024]{1,0:T(8,128)(2,1)S(1)}, u32[]{:S(2)}, u32[]{:S(2)}) collective-permute-start(bf16[32,1024]{1,0:T(8,128)(2,1)} %get-tuple-element.29.one_ref), channel_id=1, source_target_pairs={{0,224},{32,0},{64,32},{96,64},{128,96},{160,128},{192,160},{224,1... | collective-permute-start | bytes 196616 | tf_op jit(solution)/shard_map/ppermute | solution.py:31
  18.5 6.4 %collective-permute-start.9 = (bf16[32,1024]{1,0:T(8,128)(2,1)}, bf16[32,1024]{1,0:T(8,128)(2,1)S(1)}, u32[]{:S(2)}, u32[]{:S(2)}) collective-permute-start(bf16[32,1024]{1,0:T(8,128)(2,1)} %get-tuple-element.29.one_ref), channel_id=1, source_target_pairs={{0,32},{32,64},{64,96},{96,128},{128,160},{160,192},{192,224},{224... | collective-permute-start | bytes 196616 | tf_op jit(solution)/shard_map/ppermute | solution.py:31
  18.5 10.9 %collective-permute-start.11 = (bf16[32,1024]{1,0:T(8,128)(2,1)}, bf16[32,1024]{1,0:T(8,128)(2,1)S(1)}, u32[]{:S(2)}, u32[]{:S(2)}) collective-permute-start(bf16[32,1024]{1,0:T(8,128)(2,1)} %get-tuple-element.29.one_ref), channel_id=1, source_target_pairs={{0,128},{32,160},{64,192},{96,224},{128,0},{160,32},{192,64},{224,... | collective-permute-start | bytes 196616 | tf_op jit(solution)/shard_map/ppermute | solution.py:31
  25.8 7.2 %collective-permute-start.13 = (bf16[2,32,1024]{2,1,0:T(8,128)(2,1)S(1)}, bf16[2,32,1024]{2,1,0:T(8,128)(2,1)S(1)}, u32[]{:S(2)}, u32[]{:S(2)}) collective-permute-start(bf16[2,32,1024]{2,1,0:T(8,128)(2,1)S(1)} %get-tuple-element.43), channel_id=1, source_target_pairs={{0,192},{32,224},{64,0},{96,32},{128,64},{160,96},{192,128},{224,1... | collective-permute-start | bytes 393224 | tf_op jit(solution)/shard_map/ppermute | solution.py:31
  25.9 9.2 %collective-permute-start.12 = (bf16[2,32,1024]{2,1,0:T(8,128)(2,1)S(1)}, bf16[2,32,1024]{2,1,0:T(8,128)(2,1)S(1)}, u32[]{:S(2)}, u32[]{:S(2)}) collective-permute-start(bf16[2,32,1024]{2,1,0:T(8,128)(2,1)S(1)} %get-tuple-element.44), channel_id=1, source_target_pairs={{0,64},{32,96},{64,128},{96,160},{128,192},{160,224},{192,0},{224,... | collective-permute-start | bytes 393224 | tf_op jit(solution)/shard_map/ppermute | solution.py:31
  37.8 83.5 %collective-permute-start.8 = (bf16[384,4096]{1,0:T(8,128)(2,1)}, bf16[384,4096]{1,0:T(8,128)(2,1)S(1)}, u32[]{:S(2)}, u32[]{:S(2)}) collective-permute-start(bf16[384,4096]{1,0:T(8,128)(2,1)} %bitcast.61), channel_id=1, source_target_pairs={{0,1},{1,0},{2,3},{3,2},{4,5},{5,4},{6,7},{7,6},{8,9},{9,8},{10,11... | collective-permute-start | bytes 9437192 | tf_op jit(solution)/shard_map/ppermute | solution.py:31
  42.4 20.9 %all-to-all-start = ((bf16[16,32,512]{2,1,0:T(8,128)(2,1)}), bf16[16,32,512]{2,1,0:T(8,128)(2,1)}, u32[]{:S(2)}, u32[]{:S(2)}) async-start(bf16[16,32,512]{2,1,0:T(8,128)(2,1)} %get-tuple-element.24), calls=%async_computation | async-start | bytes 1048576 | tf_op jit(solution)/shard_map/all_to_all | solution.py:327
  63.3 11.9 %collective-permute-start.3 = (bf16[512,512]{1,0:T(8,128)(2,1)}, bf16[512,512]{1,0:T(8,128)(2,1)}, u32[]{:S(2)}, u32[]{:S(2)}) collective-permute-start(bf16[512,512]{1,0:T(8,128)(2,1)} %bitcast.1.refs_0_), channel_id=1, source_target_pairs={{0,224},{32,0},{64,32},{96,64},{128,96},{160,128},{192,160},{224,1... | collective-permute-start | bytes 1572872 | tf_op jit(solution)/shard_map/ppermute | solution.py:31
  63.3 13.4 %collective-permute-start.1 = (bf16[512,512]{1,0:T(8,128)(2,1)}, bf16[512,512]{1,0:T(8,128)(2,1)}, u32[]{:S(2)}, u32[]{:S(2)}) collective-permute-start(bf16[512,512]{1,0:T(8,128)(2,1)} %bitcast.1.refs_0_), channel_id=1, source_target_pairs={{0,32},{32,64},{64,96},{96,128},{128,160},{160,192},{192,224},{224... | collective-permute-start | bytes 1572872 | tf_op jit(solution)/shard_map/ppermute | solution.py:31
  75.2 21.2 %collective-permute-start.4 = (bf16[512,512]{1,0:T(8,128)(2,1)}, bf16[512,512]{1,0:T(8,128)(2,1)}, u32[]{:S(2)}, u32[]{:S(2)}) collective-permute-start(bf16[512,512]{1,0:T(8,128)(2,1)} %collective-permute-done.3.refs_2_), channel_id=1, source_target_pairs={{0,224},{32,0},{64,32},{96,64},{128,96},{160,128},{192,160},{224,1... | collective-permute-start | bytes 1572872 | tf_op jit(solution)/shard_map/ppermute | solution.py:31
  76.7 19.7 %collective-permute-start.2 = (bf16[512,512]{1,0:T(8,128)(2,1)}, bf16[512,512]{1,0:T(8,128)(2,1)}, u32[]{:S(2)}, u32[]{:S(2)}) collective-permute-start(bf16[512,512]{1,0:T(8,128)(2,1)} %collective-permute-done.1.refs_1_), channel_id=1, source_target_pairs={{0,32},{32,64},{64,96},{96,128},{128,160},{160,192},{192,224},{224... | collective-permute-start | bytes 1572872 | tf_op jit(solution)/shard_map/ppermute | solution.py:31
  77.6 16.2 %all-to-all-start.1 = ((s32[32,1,24]{2,1,0:T(1,128)}), s32[32,1,24]{2,1,0:T(1,128)S(1)}, u32[]{:S(2)}, u32[]{:S(2)}) async-start(s32[32,1,24]{2,1,0:T(1,128)} %bitcast.3), calls=%async_computation.1 | async-start | bytes 32768 | tf_op jit(solution)/shard_map/all_to_all | solution.py:339
  86.6 9.0 %collective-permute-start.7 = (s32[4,384]{1,0:T(4,128)S(1)}, s32[4,384]{1,0:T(4,128)S(1)}, u32[]{:S(2)}, u32[]{:S(2)}) collective-permute-start(s32[4,384]{1,0:T(4,128)S(1)} %get-tuple-element.49), channel_id=1, source_target_pairs={{0,1},{1,0},{2,3},{3,2},{4,5},{5,4},{6,7},{7,6},{8,9},{9,8},{10,11... | collective-permute-start | bytes 18440 | tf_op jit(solution)/shard_map/ppermute | solution.py:31
  96.2 37.5 %copy-start.15 = (s32[2,1,384]{2,1,0:T(1,128)}, s32[2,1,384]{2,1,0:T(1,128)S(1)}, u32[]{:S(2)}) copy-start(s32[2,1,384]{2,1,0:T(1,128)S(1)} %get-tuple-element.36.segr_ref) | copy-start | bytes 9220
  96.3 14.5 %collective-permute-start.5 = (bf16[512,512]{1,0:T(8,128)(2,1)}, bf16[512,512]{1,0:T(8,128)(2,1)S(1)}, u32[]{:S(2)}, u32[]{:S(2)}) collective-permute-start(bf16[512,512]{1,0:T(8,128)(2,1)} %collective-permute-done.2.refs_3_), channel_id=1, source_target_pairs={{0,32},{32,64},{64,96},{96,128},{128,160},{160,192},{192,224},{224... | collective-permute-start | bytes 1572872 | tf_op jit(solution)/shard_map/ppermute | solution.py:31
  96.4 14.4 %collective-permute-start.6 = (bf16[512,512]{1,0:T(8,128)(2,1)}, bf16[512,512]{1,0:T(8,128)(2,1)S(1)}, u32[]{:S(2)}, u32[]{:S(2)}) collective-permute-start(bf16[512,512]{1,0:T(8,128)(2,1)} %collective-permute-done.4.refs_4_), channel_id=1, source_target_pairs={{0,224},{32,0},{64,32},{96,64},{128,96},{160,128},{192,160},{224,1... | collective-permute-start | bytes 1572872 | tf_op jit(solution)/shard_map/ppermute | solution.py:31
  110.9 6.6 %collective-permute-start.15 = (bf16[512,256]{1,0:T(8,128)(2,1)S(1)}, bf16[512,256]{1,0:T(8,128)(2,1)S(1)}, u32[]{:S(2)}, u32[]{:S(2)}) collective-permute-start(bf16[512,256]{1,0:T(8,128)(2,1)S(1)} %slice.59), channel_id=1, source_target_pairs={{0,224},{32,0},{64,32},{96,64},{128,96},{160,128},{192,160},{224,1... | collective-permute-start | bytes 786440 | tf_op jit(solution)/shard_map/ppermute | solution.py:31
  113.4 7.2 %collective-permute-start.14 = (bf16[512,256]{1,0:T(8,128)(2,1)S(1)}, bf16[512,256]{1,0:T(8,128)(2,1)S(1)}, u32[]{:S(2)}, u32[]{:S(2)}) collective-permute-start(bf16[512,256]{1,0:T(8,128)(2,1)S(1)} %slice.58), channel_id=1, source_target_pairs={{0,32},{32,64},{64,96},{96,128},{128,160},{160,192},{192,224},{224... | collective-permute-start | bytes 786440 | tf_op jit(solution)/shard_map/ppermute | solution.py:31
  131.5 11.3 %collective-permute-start.17 = (bf16[2,384,256]{2,1,0:T(8,128)(2,1)}, bf16[2,384,256]{2,1,0:T(8,128)(2,1)S(1)}, u32[]{:S(2)}, u32[]{:S(2)}) collective-permute-start(bf16[2,384,256]{2,1,0:T(8,128)(2,1)} %get-tuple-element.38.cur_ref), channel_id=1, source_target_pairs={{0,2},{2,4},{4,6},{6,8},{8,10},{10,12},{12,14},{14,16},{16,18},{18... | collective-permute-start | bytes 1179656 | tf_op jit(solution)/shard_map/ppermute | solution.py:352
  153.3 44.7 %all-to-all-start.3 = ((bf16[32,48,512]{2,1,0:T(8,128)(2,1)}), bf16[32,48,512]{2,1,0:T(8,128)(2,1)S(1)}, u32[]{:S(2)}, u32[]{:S(2)}) async-start(bf16[32,48,512]{2,1,0:T(8,128)(2,1)} %bitcast.66), calls=%async_computation.3 | async-start | bytes 3145728 | tf_op jit(solution)/shard_map/all_to_all | solution.py:359
  162.0 25.5 %collective-permute-start.16 = (bf16[2,384,256]{2,1,0:T(8,128)(2,1)S(1)}, bf16[2,384,256]{2,1,0:T(8,128)(2,1)S(1)}, u32[]{:S(2)}, u32[]{:S(2)}) collective-permute-start(bf16[2,384,256]{2,1,0:T(8,128)(2,1)S(1)} %copy-done.5), channel_id=1, source_target_pairs={{0,2},{2,4},{4,6},{6,8},{8,10},{10,12},{12,14},{14,16},{16,18},{18... | collective-permute-start | bytes 1179656 | tf_op jit(solution)/shard_map/ppermute | solution.py:352
  199.2 31.4 %all-to-all-start.2 = ((bf16[32,48,512]{2,1,0:T(8,128)(2,1)}), bf16[32,48,512]{2,1,0:T(8,128)(2,1)S(1)}, u32[]{:S(2)}, u32[]{:S(2)}) async-start(bf16[32,48,512]{2,1,0:T(8,128)(2,1)} %bitcast.67), calls=%async_computation.2 | async-start | bytes 3145728 | tf_op jit(solution)/shard_map/all_to_all | solution.py:359
  (19 other events, 148.4 us)
Sparse Core Ops, SparseCore 0:
  37.9 75.7 all-gather.1

commit v3 on v2

--- a/solution.py
+++ b/solution.py
@@ -182,7 +182,7 @@
 
 
 def attend_kernel(
-    info_ref, q_ref, cur_ref, prev_ref, segc_ref, segr_ref, slot_ref, out_ref, kv_ref, bias_ref, rows_ref
+    info_ref, q_ref, cur_ref, prev_ref, segr_ref, slot_ref, out_ref, kv_ref, bias_ref, rows_ref
 ):
     b = pl.program_id(0)
     core = info_ref[0]
@@ -198,8 +198,8 @@
                 kv_ref[m, :, 2 * HEAD_DIM :] = jnp.ones((TOK, HEAD_DIM), bf16)
 
     prefix = info_ref[1 + i]
-    segc = segc_ref[i]
     segr = segr_ref[i]
+    segc = jnp.broadcast_to(segr.astype(f32), (128, TOK)).T[:, :1].astype(jnp.int32)
     leading = segc == segr[:, :1]
     row = lax.broadcasted_iota(jnp.int32, (TOK, TOK), 0)
     col = lax.broadcasted_iota(jnp.int32, (TOK, TOK), 1)
@@ -228,7 +228,7 @@
     out_ref[:, 0] = packed.reshape(DEV, CAP, GROUP * HEAD_DIM).astype(bf16)
 
 
-def attend(q, cur, prev, info, segc, segr, slot):
+def attend(q, cur, prev, info, segr, slot):
     width = GROUP * HEAD_DIM
 
     def whole(x):
@@ -241,7 +241,7 @@
             num_scalar_prefetch=1,
             grid=(2,),
             in_specs=[
-                whole(q), whole(cur), whole(prev), whole(segc), whole(segr), whole(slot),
+                whole(q), whole(cur), whole(prev), whole(segr), whole(slot),
             ],
             out_specs=pl.BlockSpec((DEV, 1, CAP, width), lambda b, info: (0, b, 0, 0)),
             scratch_shapes=[
@@ -252,7 +252,7 @@
         ),
         cost_estimate=SMALL,
         name="attend",
-    )(info, q, cur, prev, segc, segr, slot)
+    )(info, q, cur, prev, segr, slot)
 
 
 def place_kernel(places_ref, got_ref, *refs):
@@ -317,7 +317,7 @@
     cosine = jnp.concatenate([cosine, cosine], axis=2)
     sine = jnp.concatenate([-sine, sine], axis=2)
     info = jnp.concatenate([core.reshape(1).astype(jnp.int32), prefixes[:, 0]])
-    segc, segr, slots = segs[:, :, None], segs[:, None, :], slots[:, None, :]
+    segr, slots = segs[:, None, :], slots[:, None, :]
 
     zi = lax.axis_index("dp").astype(jnp.int32)
     z_ab = (zi - jnp.array(OFFSETS_Z, jnp.int32)) % NZ
@@ -343,7 +343,7 @@
     c2.append(shift(c1[1], "dp", NZ, -1))
     c2, places = tie((c2, places))
     c3 = each(c2, "dp", NZ)
-    c3, segc, segr, slots, info, cosine, sine = tie((c3, segc, segr, slots, info, cosine, sine))
+    c3, segr, slots, info, cosine, sine = tie((c3, segr, slots, info, cosine, sine))
     c4 = each([c3[0][:, :HALF], c3[1][:, HALF:]], "dp", NZ)
     cur = project_kv(lanes, own, other, c0, *c1, *c2, *c3, *c4, cosine, sine)
     onward = [(i, i + 1) for i in range(NCHIP - 1)]
@@ -355,7 +355,7 @@
     whole = []
     for head in range(2):
         q = project_q(head, own, other, wq, cosine, sine)
-        packed = attend(q, cur[head], prev[head], info, segc, segr, slots)
+        packed = attend(q, cur[head], prev[head], info, segr, slots)
         got = lax.all_to_all(
             packed.reshape(DEV, NC * CAP, PART), plane, split_axis=0, concat_axis=0, tiled=True
         ).reshape(NCHIP, NC, NC * CAP, PART)

time: 242 us -> 242 us (level)
    unnamed x42 -> x40, local copies, waits for them, and re-layouts: 7.56 us -> 7.6 us
  transfers between devices with their start and end apart: 23 -> 23, of which waited for: 12 -> 12; matrix products, arithmetic and copies ran while one was open for 6% -> 5% of each run, Pallas kernels for 16% -> 16%
where the time goes in v3:
time: 242 us; the launch traced here: 241 us
  waiting for transfers between devices  89.2 us (37%)
  starting transfers between devices  60.9 us (25%)
  Pallas kernels  55.6 us (23%)
  between operations  14.3 us (6%)
  local copies, waits for them, and re-layouts  10.6 us (4%)
  other arithmetic  10.5 us (4%)
    ppermute x16, waiting for transfers between devices, shift(): return lax.ppermute(x, axis, [(i, (i + d) % n) for i in range(n)])  34.6 us
    ppermute x16, starting transfers between devices, shift(): return lax.ppermute(x, axis, [(i, (i + d) % n) for i in range(n)])  22.4 us
    all_to_all x2, waiting for transfers between devices, on_device(): lax.all_to_all(packed.reshape(DEV, NC * CAP, PART), plane, split_axis=0,...  19.7 us
    pallas_call x2, Pallas kernels, attend(): pl.pallas_call(attend_kernel, out_shape=jax.ShapeDtypeStruct((DEV, 2, CAP...  19.5 us
    all_to_all x2, starting transfers between devices, on_device(): lax.all_to_all(packed.reshape(DEV, NC * CAP, PART), plane, split_axis=0,...  17.5 us
    pallas_call x2, Pallas kernels, project_q(): pl.pallas_call(project_q_kernel, out_shape=jax.ShapeDtypeStruct((2, TOK,...  16.4 us
    all_to_all x1, waiting for transfers between devices, on_device(): c0 = lax.all_to_all(wc, chips, split_axis=0, concat_axis=0, tiled=True)  14.3 us
    ppermute x2, waiting for transfers between devices, on_device(): prev.append(lax.ppermute(cur[h], chips, onward))  13.8 us
  transfers between devices with their start and end apart: 23, of which 12 were waited for; matrix products, arithmetic and copies ran while one was open for 5% of the time, Pallas kernels for 16%

profile of v3, /device:TPU:1, one launch (start us, length us, event | category | flops | bytes accessed | tf_op | source)
XLA Modules:
  0.0 241.1 jit_solution(13654197630685065593)
XLA Ops:
  8.1 3.2 %collective-permute-start = (bf16[16,1536]{1,0:T(8,128)(2,1)}, bf16[16,1536]{1,0:T(8,128)(2,1)S(1)}, u32[]{:S(2)}, u32[]{:S(2)}) collective-permute-start(bf16[16,1536]{1,0:T(8,128)(2,1)} %get-tuple-element.22), channel_id=1, source_target_pairs={{0,1},{1,0},{2,3},{3,2},{4,5},{5,4},{6,7},{7,6},{8,9},{9,8},{10,11... | collective-permute-start | bytes 147464 | tf_op jit(solution)/shard_map/ppermute | solution.py:31
  14.7 3.9 %collective-permute-start.10 = (bf16[32,1024]{1,0:T(8,128)(2,1)}, bf16[32,1024]{1,0:T(8,128)(2,1)S(1)}, u32[]{:S(2)}, u32[]{:S(2)}) collective-permute-start(bf16[32,1024]{1,0:T(8,128)(2,1)} %get-tuple-element.28.one_ref), channel_id=1, source_target_pairs={{0,224},{32,0},{64,32},{96,64},{128,96},{160,128},{192,160},{224,1... | collective-permute-start | bytes 196616 | tf_op jit(solution)/shard_map/ppermute | solution.py:31
  21.4 3.6 %collective-permute-done.9.up_ref = bf16[32,1024]{1,0:T(8,128)(2,1)S(1)} collective-permute-done((bf16[32,1024]{1,0:T(8,128)(2,1)}, bf16[32,1024]{1,0:T(8,128)(2,1)S(1)}, u32[]{:S(2)}, u32[]{:S(2)}) %collective-permute-start.9) | collective-permute-done | bytes 65568 | tf_op jit(solution)/shard_map/ppermute | solution.py:31
  29.5 3.5 %collective-permute-done.13.down2_ref = bf16[2,32,1024]{2,1,0:T(8,128)(2,1)S(1)} collective-permute-done((bf16[2,32,1024]{2,1,0:T(8,128)(2,1)S(1)}, bf16[2,32,1024]{2,1,0:T(8,128)(2,1)S(1)}, u32[]{:S(2)}, u32[]{:S(2)}) %collective-permute-start.13) | collective-permute-done | bytes 131104 | tf_op jit(solution)/shard_map/ppermute | solution.py:31
  42.4 6.8 %all-to-all-start = ((bf16[16,32,512]{2,1,0:T(8,128)(2,1)}), bf16[16,32,512]{2,1,0:T(8,128)(2,1)}, u32[]{:S(2)}, u32[]{:S(2)}) async-start(bf16[16,32,512]{2,1,0:T(8,128)(2,1)} %get-tuple-element.23), calls=%async_computation | async-start | bytes 1048576 | tf_op jit(solution)/shard_map/all_to_all | solution.py:327
  49.4 14.3 %all-to-all-done = bf16[16,32,512]{2,1,0:T(8,128)(2,1)} async-done(((bf16[16,32,512]{2,1,0:T(8,128)(2,1)}), bf16[16,32,512]{2,1,0:T(8,128)(2,1)}, u32[]{:S(2)}, u32[]{:S(2)}) %all-to-all-start) | async-done | bytes 524320 | tf_op jit(solution)/shard_map/all_to_all | solution.py:327
  66.0 9.9 %collective-permute-done.3.refs_2_ = bf16[512,512]{1,0:T(8,128)(2,1)} collective-permute-done((bf16[512,512]{1,0:T(8,128)(2,1)}, bf16[512,512]{1,0:T(8,128)(2,1)}, u32[]{:S(2)}, u32[]{:S(2)}) %collective-permute-start.3) | collective-permute-done | bytes 524320 | tf_op jit(solution)/shard_map/ppermute | solution.py:31
  78.3 8.5 %all-to-all-start.1 = ((s32[32,1,24]{2,1,0:T(1,128)}), s32[32,1,24]{2,1,0:T(1,128)S(1)}, u32[]{:S(2)}, u32[]{:S(2)}) async-start(s32[32,1,24]{2,1,0:T(1,128)} %bitcast.3), calls=%async_computation.1 | async-start | bytes 32768 | tf_op jit(solution)/shard_map/all_to_all | solution.py:339
  87.2 6.8 %all-to-all-done.1 = s32[32,1,24]{2,1,0:T(1,128)S(1)} async-done(((s32[32,1,24]{2,1,0:T(1,128)}), s32[32,1,24]{2,1,0:T(1,128)S(1)}, u32[]{:S(2)}, u32[]{:S(2)}) %all-to-all-start.1) | async-done | bytes 3104 | tf_op jit(solution)/shard_map/all_to_all | solution.py:339
  103.2 7.9 %collective-permute-done.5.refs_5_ = bf16[512,512]{1,0:T(8,128)(2,1)S(1)} collective-permute-done((bf16[512,512]{1,0:T(8,128)(2,1)}, bf16[512,512]{1,0:T(8,128)(2,1)S(1)}, u32[]{:S(2)}, u32[]{:S(2)}) %collective-permute-start.5) | collective-permute-done | bytes 524320 | tf_op jit(solution)/shard_map/ppermute | solution.py:31
  114.2 3.5 %collective-permute-done.15.refs_8_ = bf16[512,256]{1,0:T(8,128)(2,1)S(1)} collective-permute-done((bf16[512,256]{1,0:T(8,128)(2,1)S(1)}, bf16[512,256]{1,0:T(8,128)(2,1)S(1)}, u32[]{:S(2)}, u32[]{:S(2)}) %collective-permute-start.15) | collective-permute-done | bytes 262176 | tf_op jit(solution)/shard_map/ppermute | solution.py:31
  117.8 3.1 %collective-permute-done.14.refs_7_ = bf16[512,256]{1,0:T(8,128)(2,1)S(1)} collective-permute-done((bf16[512,256]{1,0:T(8,128)(2,1)S(1)}, bf16[512,256]{1,0:T(8,128)(2,1)S(1)}, u32[]{:S(2)}, u32[]{:S(2)}) %collective-permute-start.14) | collective-permute-done | bytes 262176 | tf_op jit(solution)/shard_map/ppermute | solution.py:31
  123.3 8.6 %project_kv.1 = (bf16[2,384,256]{2,1,0:T(8,128)(2,1)}, bf16[2,384,256]{2,1,0:T(8,128)(2,1)}) custom-call(s32[8]{0:T(128)} %fusion.14.lane_ref, bf16[384,4096]{1,0:T(8,128)(2,1)} %bitcast.61, bf16[384,4096]{1,0:T(8,128)(2,1)} %copy-done, bf16[512,512]{1,0:T(8,128)(2,1)} %bitcast.1.refs_0_, bf16[512,512]{1,0:T(8,128)(2,1)} %collective-permute-done.1.refs_1_, ...), custom_call_target="tpu_custom_call" | custom-call | flops 1048576 | bytes 1048576 | tf_op jit(solution)/shard_map/project_kv/pallas_call | solution.py:141
  134.1 8.1 %project_q.3.q_ref = bf16[2,384,512]{2,1,0:T(8,128)(2,1)} custom-call(bf16[384,4096]{1,0:T(8,128)(2,1)} %bitcast.62, bf16[384,4096]{1,0:T(8,128)(2,1)} %copy-done, bf16[16,8,32,1024]{3,2,1,0:T(8,128)(2,1)} %bitcast.58, f32[2,384,128]{2,1,0:T(8,128)} %pad_maximum_fusion.cos_ref.refs_9_, f32[2,384,128]{2,1,0:T(8,128)} %pad_maximum_fusion.1.sin_ref.refs_10_), custom_call_target="tpu_custom_call" | custom-call | flops 1048576 | bytes 1048576 | tf_op jit(solution)/shard_map/project_q/pallas_call | solution.py:167
  143.0 9.7 %attend.3 = bf16[32,2,24,512]{3,2,1,0:T(8,128)(2,1)} custom-call(s32[3]{0:T(128)} %pad_add_fusion.2.info_ref, bf16[2,384,512]{2,1,0:T(8,128)(2,1)} %project_q.3.q_ref, bf16[2,384,256]{2,1,0:T(8,128)(2,1)} %get-tuple-element.36.cur_ref, bf16[2,384,256]{2,1,0:T(8,128)(2,1)} %copy-done.7, s32[2,1,384]{2,1,0:T(1,128)} %get-tuple-element.34.segr_ref, ...), custom_call_target="tpu_custom_call" | custom-call | flops 1048576 | bytes 1048576 | tf_op jit(solution)/shard_map/attend/pallas_call | solution.py:237
  152.8 8.7 %all-to-all-start.3 = ((bf16[32,48,512]{2,1,0:T(8,128)(2,1)}), bf16[32,48,512]{2,1,0:T(8,128)(2,1)S(1)}, u32[]{:S(2)}, u32[]{:S(2)}) async-start(bf16[32,48,512]{2,1,0:T(8,128)(2,1)} %bitcast.65), calls=%async_computation.3 | async-start | bytes 3145728 | tf_op jit(solution)/shard_map/all_to_all | solution.py:359
  161.5 3.5 %collective-permute-start.16 = (bf16[2,384,256]{2,1,0:T(8,128)(2,1)S(1)}, bf16[2,384,256]{2,1,0:T(8,128)(2,1)S(1)}, u32[]{:S(2)}, u32[]{:S(2)}) collective-permute-start(bf16[2,384,256]{2,1,0:T(8,128)(2,1)S(1)} %copy-done.5), channel_id=1, source_target_pairs={{0,2},{2,4},{4,6},{6,8},{8,10},{10,12},{12,14},{14,16},{16,18},{18... | collective-permute-start | bytes 1179656 | tf_op jit(solution)/shard_map/ppermute | solution.py:352
  165.0 8.2 %project_q.2.q_ref = bf16[2,384,512]{2,1,0:T(8,128)(2,1)} custom-call(bf16[384,4096]{1,0:T(8,128)(2,1)} %bitcast.63, bf16[384,4096]{1,0:T(8,128)(2,1)} %copy-done, bf16[16,8,32,1024]{3,2,1,0:T(8,128)(2,1)} %bitcast.59, f32[2,384,128]{2,1,0:T(8,128)} %pad_maximum_fusion.cos_ref.refs_9_, f32[2,384,128]{2,1,0:T(8,128)} %pad_maximum_fusion.1.sin_ref.refs_10_), custom_call_target="tpu_custom_call" | custom-call | flops 1048576 | bytes 1048576 | tf_op jit(solution)/shard_map/project_q/pallas_call | solution.py:167
  173.2 13.8 %collective-permute-done.16.prev_ref = bf16[2,384,256]{2,1,0:T(8,128)(2,1)S(1)} collective-permute-done((bf16[2,384,256]{2,1,0:T(8,128)(2,1)S(1)}, bf16[2,384,256]{2,1,0:T(8,128)(2,1)S(1)}, u32[]{:S(2)}, u32[]{:S(2)}) %collective-permute-start.16) | collective-permute-done | bytes 393248 | tf_op jit(solution)/shard_map/ppermute | solution.py:352
  187.8 9.8 %attend.2 = bf16[32,2,24,512]{3,2,1,0:T(8,128)(2,1)} custom-call(s32[3]{0:T(128)} %pad_add_fusion.2.info_ref, bf16[2,384,512]{2,1,0:T(8,128)(2,1)} %project_q.2.q_ref, bf16[2,384,256]{2,1,0:T(8,128)(2,1)} %get-tuple-element.33.cur_ref, bf16[2,384,256]{2,1,0:T(8,128)(2,1)} %copy-done.6, s32[2,1,384]{2,1,0:T(1,128)} %get-tuple-element.34.segr_ref, ...), custom_call_target="tpu_custom_call" | custom-call | flops 1048576 | bytes 1048576 | tf_op jit(solution)/shard_map/attend/pallas_call | solution.py:237
  198.7 8.8 %all-to-all-start.2 = ((bf16[32,48,512]{2,1,0:T(8,128)(2,1)}), bf16[32,48,512]{2,1,0:T(8,128)(2,1)S(1)}, u32[]{:S(2)}, u32[]{:S(2)}) async-start(bf16[32,48,512]{2,1,0:T(8,128)(2,1)} %bitcast.66), calls=%async_computation.2 | async-start | bytes 3145728 | tf_op jit(solution)/shard_map/all_to_all | solution.py:359
  207.5 3.0 %place.2.refs_0_ = bf16[384,2048]{1,0:T(8,128)(2,1)} custom-call(s32[1,768]{1,0:T(1,128)} %reshape.157.places_ref, bf16[16,2,48,512]{3,2,1,0:T(8,128)(2,1)} %bitcast.64), custom_call_target="tpu_custom_call" | custom-call | flops 1048576 | bytes 1048576 | tf_op jit(solution)/shard_map/place/pallas_call | solution.py:272
  210.5 19.7 %all-to-all-done.2 = bf16[32,48,512]{2,1,0:T(8,128)(2,1)S(1)} async-done(((bf16[32,48,512]{2,1,0:T(8,128)(2,1)}), bf16[32,48,512]{2,1,0:T(8,128)(2,1)S(1)}, u32[]{:S(2)}, u32[]{:S(2)}) %all-to-all-start.2) | async-done | bytes 1572896 | tf_op jit(solution)/shard_map/all_to_all | solution.py:359
  231.3 3.0 %place.3 = bf16[384,2048]{1,0:T(8,128)(2,1)} custom-call(s32[1,768]{1,0:T(1,128)} %reshape.157.places_ref, bf16[16,2,48,512]{3,2,1,0:T(8,128)(2,1)} %bitcast.67, bf16[384,2048]{1,0:T(8,128)(2,1)} %place.2.refs_0_), custom_call_target="tpu_custom_call", output_to_operand_aliasing={{}: (2, {})} | custom-call | flops 1048576 | bytes 1048576 | tf_op jit(solution)/shard_map/place/pallas_call | solution.py:272
  (111 shorter events, 47.1 us)
Async XLA Ops:
  6.5 34.7 %copy-start.17 = (s32[1,384]{1,0:T(1,128)S(1)}, s32[1,384]{1,0:T(1,128)}, u32[]{:S(2)}) copy-start(s32[1,384]{1,0:T(1,128)} %param.10) | copy-start | bytes 4612
  6.5 127.6 %all-gather.2.cloned.1.call-start = ((), (), s32[]{:S(2)}) async-start(), calls=%async_computation.4 | async-start | bytes 8912896 | tf_op jit(solution)/shard_map/all_gather | solution.py:335
  8.1 4.3 %collective-permute-start = (bf16[16,1536]{1,0:T(8,128)(2,1)}, bf16[16,1536]{1,0:T(8,128)(2,1)S(1)}, u32[]{:S(2)}, u32[]{:S(2)}) collective-permute-start(bf16[16,1536]{1,0:T(8,128)(2,1)} %get-tuple-element.22), channel_id=1, source_target_pairs={{0,1},{1,0},{2,3},{3,2},{4,5},{5,4},{6,7},{7,6},{8,9},{9,8},{10,11... | collective-permute-start | bytes 147464 | tf_op jit(solution)/shard_map/ppermute | solution.py:31
  14.7 6.7 %collective-permute-start.10 = (bf16[32,1024]{1,0:T(8,128)(2,1)}, bf16[32,1024]{1,0:T(8,128)(2,1)S(1)}, u32[]{:S(2)}, u32[]{:S(2)}) collective-permute-start(bf16[32,1024]{1,0:T(8,128)(2,1)} %get-tuple-element.28.one_ref), channel_id=1, source_target_pairs={{0,224},{32,0},{64,32},{96,64},{128,96},{160,128},{192,160},{224,1... | collective-permute-start | bytes 196616 | tf_op jit(solution)/shard_map/ppermute | solution.py:31
  18.5 6.4 %collective-permute-start.9 = (bf16[32,1024]{1,0:T(8,128)(2,1)}, bf16[32,1024]{1,0:T(8,128)(2,1)S(1)}, u32[]{:S(2)}, u32[]{:S(2)}) collective-permute-start(bf16[32,1024]{1,0:T(8,128)(2,1)} %get-tuple-element.28.one_ref), channel_id=1, source_target_pairs={{0,32},{32,64},{64,96},{96,128},{128,160},{160,192},{192,224},{224... | collective-permute-start | bytes 196616 | tf_op jit(solution)/shard_map/ppermute | solution.py:31
  18.6 11.0 %collective-permute-start.11 = (bf16[32,1024]{1,0:T(8,128)(2,1)}, bf16[32,1024]{1,0:T(8,128)(2,1)S(1)}, u32[]{:S(2)}, u32[]{:S(2)}) collective-permute-start(bf16[32,1024]{1,0:T(8,128)(2,1)} %get-tuple-element.28.one_ref), channel_id=1, source_target_pairs={{0,128},{32,160},{64,192},{96,224},{128,0},{160,32},{192,64},{224,... | collective-permute-start | bytes 196616 | tf_op jit(solution)/shard_map/ppermute | solution.py:31
  25.9 7.2 %collective-permute-start.13 = (bf16[2,32,1024]{2,1,0:T(8,128)(2,1)S(1)}, bf16[2,32,1024]{2,1,0:T(8,128)(2,1)S(1)}, u32[]{:S(2)}, u32[]{:S(2)}) collective-permute-start(bf16[2,32,1024]{2,1,0:T(8,128)(2,1)S(1)} %get-tuple-element.41), channel_id=1, source_target_pairs={{0,192},{32,224},{64,0},{96,32},{128,64},{160,96},{192,128},{224,1... | collective-permute-start | bytes 393224 | tf_op jit(solution)/shard_map/ppermute | solution.py:31
  25.9 9.2 %collective-permute-start.12 = (bf16[2,32,1024]{2,1,0:T(8,128)(2,1)S(1)}, bf16[2,32,1024]{2,1,0:T(8,128)(2,1)S(1)}, u32[]{:S(2)}, u32[]{:S(2)}) collective-permute-start(bf16[2,32,1024]{2,1,0:T(8,128)(2,1)S(1)} %get-tuple-element.42), channel_id=1, source_target_pairs={{0,64},{32,96},{64,128},{96,160},{128,192},{160,224},{192,0},{224,... | collective-permute-start | bytes 393224 | tf_op jit(solution)/shard_map/ppermute | solution.py:31
  37.8 83.8 %collective-permute-start.8 = (bf16[384,4096]{1,0:T(8,128)(2,1)}, bf16[384,4096]{1,0:T(8,128)(2,1)S(1)}, u32[]{:S(2)}, u32[]{:S(2)}) collective-permute-start(bf16[384,4096]{1,0:T(8,128)(2,1)} %bitcast.60), channel_id=1, source_target_pairs={{0,1},{1,0},{2,3},{3,2},{4,5},{5,4},{6,7},{7,6},{8,9},{9,8},{10,11... | collective-permute-start | bytes 9437192 | tf_op jit(solution)/shard_map/ppermute | solution.py:31
  42.4 21.2 %all-to-all-start = ((bf16[16,32,512]{2,1,0:T(8,128)(2,1)}), bf16[16,32,512]{2,1,0:T(8,128)(2,1)}, u32[]{:S(2)}, u32[]{:S(2)}) async-start(bf16[16,32,512]{2,1,0:T(8,128)(2,1)} %get-tuple-element.23), calls=%async_computation | async-start | bytes 1048576 | tf_op jit(solution)/shard_map/all_to_all | solution.py:327
  63.6 12.3 %collective-permute-start.3 = (bf16[512,512]{1,0:T(8,128)(2,1)}, bf16[512,512]{1,0:T(8,128)(2,1)}, u32[]{:S(2)}, u32[]{:S(2)}) collective-permute-start(bf16[512,512]{1,0:T(8,128)(2,1)} %bitcast.1.refs_0_), channel_id=1, source_target_pairs={{0,224},{32,0},{64,32},{96,64},{128,96},{160,128},{192,160},{224,1... | collective-permute-start | bytes 1572872 | tf_op jit(solution)/shard_map/ppermute | solution.py:31
  63.6 13.8 %collective-permute-start.1 = (bf16[512,512]{1,0:T(8,128)(2,1)}, bf16[512,512]{1,0:T(8,128)(2,1)}, u32[]{:S(2)}, u32[]{:S(2)}) collective-permute-start(bf16[512,512]{1,0:T(8,128)(2,1)} %bitcast.1.refs_0_), channel_id=1, source_target_pairs={{0,32},{32,64},{64,96},{96,128},{128,160},{160,192},{192,224},{224... | collective-permute-start | bytes 1572872 | tf_op jit(solution)/shard_map/ppermute | solution.py:31
  75.9 20.7 %collective-permute-start.4 = (bf16[512,512]{1,0:T(8,128)(2,1)}, bf16[512,512]{1,0:T(8,128)(2,1)}, u32[]{:S(2)}, u32[]{:S(2)}) collective-permute-start(bf16[512,512]{1,0:T(8,128)(2,1)} %collective-permute-done.3.refs_2_), channel_id=1, source_target_pairs={{0,224},{32,0},{64,32},{96,64},{128,96},{160,128},{192,160},{224,1... | collective-permute-start | bytes 1572872 | tf_op jit(solution)/shard_map/ppermute | solution.py:31
  77.4 19.2 %collective-permute-start.2 = (bf16[512,512]{1,0:T(8,128)(2,1)}, bf16[512,512]{1,0:T(8,128)(2,1)}, u32[]{:S(2)}, u32[]{:S(2)}) collective-permute-start(bf16[512,512]{1,0:T(8,128)(2,1)} %collective-permute-done.1.refs_1_), channel_id=1, source_target_pairs={{0,32},{32,64},{64,96},{96,128},{128,160},{160,192},{192,224},{224... | collective-permute-start | bytes 1572872 | tf_op jit(solution)/shard_map/ppermute | solution.py:31
  78.3 15.7 %all-to-all-start.1 = ((s32[32,1,24]{2,1,0:T(1,128)}), s32[32,1,24]{2,1,0:T(1,128)S(1)}, u32[]{:S(2)}, u32[]{:S(2)}) async-start(s32[32,1,24]{2,1,0:T(1,128)} %bitcast.3), calls=%async_computation.1 | async-start | bytes 32768 | tf_op jit(solution)/shard_map/all_to_all | solution.py:339
  86.8 9.0 %collective-permute-start.7 = (s32[4,384]{1,0:T(4,128)S(1)}, s32[4,384]{1,0:T(4,128)S(1)}, u32[]{:S(2)}, u32[]{:S(2)}) collective-permute-start(s32[4,384]{1,0:T(4,128)S(1)} %get-tuple-element.47), channel_id=1, source_target_pairs={{0,1},{1,0},{2,3},{3,2},{4,5},{5,4},{6,7},{7,6},{8,9},{9,8},{10,11... | collective-permute-start | bytes 18440 | tf_op jit(solution)/shard_map/ppermute | solution.py:31
  96.6 14.5 %collective-permute-start.5 = (bf16[512,512]{1,0:T(8,128)(2,1)}, bf16[512,512]{1,0:T(8,128)(2,1)S(1)}, u32[]{:S(2)}, u32[]{:S(2)}) collective-permute-start(bf16[512,512]{1,0:T(8,128)(2,1)} %collective-permute-done.2.refs_3_), channel_id=1, source_target_pairs={{0,32},{32,64},{64,96},{96,128},{128,160},{160,192},{192,224},{224... | collective-permute-start | bytes 1572872 | tf_op jit(solution)/shard_map/ppermute | solution.py:31
  96.7 14.4 %collective-permute-start.6 = (bf16[512,512]{1,0:T(8,128)(2,1)}, bf16[512,512]{1,0:T(8,128)(2,1)S(1)}, u32[]{:S(2)}, u32[]{:S(2)}) collective-permute-start(bf16[512,512]{1,0:T(8,128)(2,1)} %collective-permute-done.4.refs_4_), channel_id=1, source_target_pairs={{0,224},{32,0},{64,32},{96,64},{128,96},{160,128},{192,160},{224,1... | collective-permute-start | bytes 1572872 | tf_op jit(solution)/shard_map/ppermute | solution.py:31
  111.2 6.6 %collective-permute-start.15 = (bf16[512,256]{1,0:T(8,128)(2,1)S(1)}, bf16[512,256]{1,0:T(8,128)(2,1)S(1)}, u32[]{:S(2)}, u32[]{:S(2)}) collective-permute-start(bf16[512,256]{1,0:T(8,128)(2,1)S(1)} %slice.59), channel_id=1, source_target_pairs={{0,224},{32,0},{64,32},{96,64},{128,96},{160,128},{192,160},{224,1... | collective-permute-start | bytes 786440 | tf_op jit(solution)/shard_map/ppermute | solution.py:31
  113.6 7.2 %collective-permute-start.14 = (bf16[512,256]{1,0:T(8,128)(2,1)S(1)}, bf16[512,256]{1,0:T(8,128)(2,1)S(1)}, u32[]{:S(2)}, u32[]{:S(2)}) collective-permute-start(bf16[512,256]{1,0:T(8,128)(2,1)S(1)} %slice.58), channel_id=1, source_target_pairs={{0,32},{32,64},{64,96},{96,128},{128,160},{160,192},{192,224},{224... | collective-permute-start | bytes 786440 | tf_op jit(solution)/shard_map/ppermute | solution.py:31
  131.8 10.4 %collective-permute-start.17 = (bf16[2,384,256]{2,1,0:T(8,128)(2,1)}, bf16[2,384,256]{2,1,0:T(8,128)(2,1)S(1)}, u32[]{:S(2)}, u32[]{:S(2)}) collective-permute-start(bf16[2,384,256]{2,1,0:T(8,128)(2,1)} %get-tuple-element.36.cur_ref), channel_id=1, source_target_pairs={{0,2},{2,4},{4,6},{6,8},{8,10},{10,12},{12,14},{14,16},{16,18},{18... | collective-permute-start | bytes 1179656 | tf_op jit(solution)/shard_map/ppermute | solution.py:352
  152.8 44.8 %all-to-all-start.3 = ((bf16[32,48,512]{2,1,0:T(8,128)(2,1)}), bf16[32,48,512]{2,1,0:T(8,128)(2,1)S(1)}, u32[]{:S(2)}, u32[]{:S(2)}) async-start(bf16[32,48,512]{2,1,0:T(8,128)(2,1)} %bitcast.65), calls=%async_computation.3 | async-start | bytes 3145728 | tf_op jit(solution)/shard_map/all_to_all | solution.py:359
  161.5 25.5 %collective-permute-start.16 = (bf16[2,384,256]{2,1,0:T(8,128)(2,1)S(1)}, bf16[2,384,256]{2,1,0:T(8,128)(2,1)S(1)}, u32[]{:S(2)}, u32[]{:S(2)}) collective-permute-start(bf16[2,384,256]{2,1,0:T(8,128)(2,1)S(1)} %copy-done.5), channel_id=1, source_target_pairs={{0,2},{2,4},{4,6},{6,8},{8,10},{10,12},{12,14},{14,16},{16,18},{18... | collective-permute-start | bytes 1179656 | tf_op jit(solution)/shard_map/ppermute | solution.py:352
  198.7 31.4 %all-to-all-start.2 = ((bf16[32,48,512]{2,1,0:T(8,128)(2,1)}), bf16[32,48,512]{2,1,0:T(8,128)(2,1)S(1)}, u32[]{:S(2)}, u32[]{:S(2)}) async-start(bf16[32,48,512]{2,1,0:T(8,128)(2,1)} %bitcast.66), calls=%async_computation.2 | async-start | bytes 3145728 | tf_op jit(solution)/shard_map/all_to_all | solution.py:359
  (18 other events, 113.8 us)
Sparse Core Ops, SparseCore 0:
  37.9 75.7 all-gather.1
